TPU v7x, 512 devices: a whole 4x8x8 slice. The times are simulated.
512 devices in a mesh: row: 32 (over x_hi, y, core), frame: 16 (over z, x_lo).
Axes of the slice: x: 4 (x_hi: 2, x_lo: 2; x = x_hi * 2 + x_lo), y: 8, z: 8, core: 2. Of those that a mesh axis runs over, the one named last changes fastest.
Arguments:
- frames: bfloat16 [64, 64, 256, 128], P('frame', None, 'row'), may hold values from -6 to 6
- w_pair: bfloat16 [3, 3, 64, 128], replicated, may hold values from -0.1875 to 0.1875
- w_mixed: bfloat16 [3, 3, 64, 64], replicated, may hold values from -0.25 to 0.25
- slope_pair: float32 [64], replicated, may hold values from 0.05 to 0.5
- slope_mixed: float32 [64], replicated, may hold values from 0.05 to 0.5
Outputs:
- merged: bfloat16 [16, 64, 256, 128], P('frame', None, 'row')
All inputs are finite; a program needn't handle non-finite values.
Results may differ from a plain program's by a relative error of at most 0.0051.
Values may be sent and summed in bfloat16 or wider, within the bound.
No kernel may reach another device: no remote copies, remote signals or barrier semaphores. Data moves between devices by JAX's collectives and lax.ppermute only.
A program may use at most 64 MiB of HBM per device.

v0:
```python
import jax
import jax.numpy as jnp
from jax import lax
from jax.experimental import pallas as pl
from jax.experimental.pallas import tpu as pltpu
from jax.sharding import PartitionSpec as P


ROWS = 8
HALO = 4
CH = 64
LANES = 128
VMEM = pl.BlockSpec(memory_space=pltpu.VMEM)
SMALL = pltpu.CompilerParams(vmem_limit_bytes=8 << 20)


def array(*shape, dtype=jnp.bfloat16):
    return jax.ShapeDtypeStruct(shape, dtype)


def position():
    return lax.axis_index("frame") // (lax.axis_size("frame") // 4)


def spread(frames):
    def body(src, own, one, three, two, wide):
        at = position()
        for k, out in ((2, two), (1, one), (3, three), (0, own)):
            wide[k] = src[at ^ k].astype(jnp.float32).reshape(CH * ROWS, LANES)
            for row in range(ROWS):
                out[row] = wide[k, pl.ds(row, CH, stride=ROWS), :].astype(jnp.bfloat16)

    return pl.pallas_call(
        body,
        out_shape=(array(ROWS, CH, LANES),) * 4,
        in_specs=[VMEM],
        out_specs=(VMEM,) * 4,
        scratch_shapes=[pltpu.VMEM((4, CH * ROWS, LANES), jnp.float32)],
        compiler_params=SMALL,
        name="spread",
    )(frames)


def weights(w_pair, w_mixed, slope_pair, slope_mixed):
    def body(wp, wm, sp, sm, pair, mixed, cols):
        for ky in range(3):
            at = ky * 2 * CH
            pair[0, :, at : at + 2 * CH] = wp[ky]
            pair[1, :, at : at + 2 * CH] = jnp.concatenate([wp[ky][:, CH:], wp[ky][:, :CH]], axis=1)
        mixed[...] = jnp.concatenate([wm[0], wm[1], wm[2]], axis=1)
        square = lax.broadcasted_iota(jnp.int32, (CH, CH), 0) == lax.broadcasted_iota(jnp.int32, (CH, CH), 1)
        for k, slope in enumerate((sp, sm)):
            column = jnp.sum(jnp.where(square, slope[...], 0.0), axis=1, keepdims=True)
            cols[k] = jnp.broadcast_to(column, (CH, LANES))

    return pl.pallas_call(
        body,
        out_shape=(array(2, 3 * CH, 6 * CH), array(3 * CH, 3 * CH), array(2, CH, LANES, dtype=jnp.float32)),
        in_specs=[VMEM] * 4,
        out_specs=(VMEM,) * 3,
        compiler_params=SMALL,
        name="weights",
    )(w_pair.reshape(3, 3 * CH, 2 * CH), w_mixed.reshape(3, 3 * CH, CH), slope_pair.reshape(1, CH), slope_mixed.reshape(1, CH))


def edges(*frames):
    def body(*refs):
        near_side, far_side = refs[-2:]
        odd = lax.axis_index("row") % 2
        for k, frame in enumerate(refs[:-2]):
            near_side[:, k * CH : (k + 1) * CH, :] = frame[pl.ds(HALO - HALO * odd, HALO)]
            far_side[:, k * CH : (k + 1) * CH, :] = frame[pl.ds(HALO * odd, HALO)]

    half = array(HALO, len(frames) * CH, LANES)
    return pl.pallas_call(
        body,
        out_shape=(half, half),
        in_specs=[VMEM] * len(frames),
        out_specs=(VMEM,) * 2,
        compiler_params=SMALL,
        name="edges",
    )(*frames)


def fill(stack, slot, near_side, frame, far_side, part):
    odd = lax.axis_index("row") % 2
    to = slice(slot * CH, (slot + 1) * CH)
    of = slice(part * CH, (part + 1) * CH)
    stack[HALO : HALO + ROWS, to, :] = frame[...]
    stack[pl.ds((HALO + ROWS) * (1 - odd), HALO), to, :] = near_side[:, of, :]
    stack[pl.ds((HALO + ROWS) * odd, HALO), to, :] = far_side[:, of, :]


class Level:
    def __init__(self, pair, mixed, cols, swap, hid):
        lane = lax.broadcasted_iota(jnp.int32, (CH, LANES), 1)
        self.not_first = lane > 0
        self.not_last = lane < LANES - 1
        self.pair = pair[swap]
        self.mixed = mixed[...]
        self.cols = cols
        self.swap = swap
        self.hid = hid
        self.place = lax.axis_index("row")
        self.last = lax.axis_size("row") - 1

    def inside(self, row, value):
        if row < HALO:
            return jnp.where(self.place > 0, value, 0.0)
        if row >= HALO + ROWS:
            return jnp.where(self.place < self.last, value, 0.0)
        return value

    def fold(self, part, which):
        left = jnp.where(self.not_first, pltpu.roll(part[:CH], 1, 1), 0.0)
        right = jnp.where(self.not_last, pltpu.roll(part[2 * CH :], LANES - 1, 1), 0.0)
        total = part[CH : 2 * CH] + left + right
        return jnp.maximum(total, self.cols[which] * total)

    def product(self, lhs, stack, row, depth):
        rhs = jnp.concatenate([stack[r - 1 : r + 2].reshape(3 * depth, LANES) for r in (row, row + 1)], axis=1)
        return jnp.dot(lhs, rhs, preferred_element_type=jnp.float32)

    def run(self, stack, shift, low, high, emit):
        for row in range(low - 1, high + 1, 2):
            both = self.product(self.pair, stack, row - shift, 2 * CH)
            for k in range(2):
                value = self.fold(both[:, k * LANES : (k + 1) * LANES], 0)
                self.hid[row + k] = self.inside(row + k, value).astype(jnp.bfloat16)
        for row in range(low, high, 2):
            both = self.product(self.mixed, self.hid, row, CH)
            for k in range(2):
                first = stack[row + k - shift, pl.ds(self.swap * CH, CH), :].astype(jnp.float32)
                branch = self.fold(both[:, k * LANES : (k + 1) * LANES], 1)
                emit(row + k, self.inside(row + k, first + branch))


def merge_own(near_side, far_side, own, two, tables):
    def body(near_r, far_r, own_r, two_r, pair, mixed, cols, out, stack, hid):
        fill(stack, 0, near_r, own_r, far_r, 0)
        fill(stack, 1, near_r, two_r, far_r, 1)

        def emit(row, value):
            out[row - 2] = value.astype(jnp.bfloat16)

        Level(pair, mixed, cols, position() // 2, hid).run(stack, 0, 2, 14, emit)

    return pl.pallas_call(
        body,
        out_shape=array(12, CH, LANES),
        in_specs=[VMEM] * 7,
        out_specs=VMEM,
        scratch_shapes=[
            pltpu.VMEM((16, 2 * CH, LANES), jnp.bfloat16),
            pltpu.VMEM((16, CH, LANES), jnp.bfloat16),
        ],
        compiler_params=SMALL,
        name="merge_own",
    )(near_side, far_side, own, two, *tables)


def merge_rest(near_side, far_side, one, three, mine, tables):
    def body(near_r, far_r, one_r, three_r, mine_r, pair, mixed, cols, out, stack, ones, hid, hid_two, wide):
        fill(stack, 0, near_r, one_r, far_r, 0)
        fill(stack, 1, near_r, three_r, far_r, 1)
        ones[:, :CH, :] = mine_r[...]
        at = position()

        def emit(row, value):
            ones[row - 2, CH:, :] = value.astype(jnp.bfloat16)

        Level(pair, mixed, cols, at // 2, hid).run(stack, 0, 2, 14, emit)

        def emit_two(row, value):
            wide[pl.ds(row - HALO, CH, stride=ROWS), :] = value

        Level(pair, mixed, cols, at % 2, hid_two).run(ones, 2, HALO, HALO + ROWS, emit_two)
        out[...] = wide[...].reshape(CH, ROWS, LANES).astype(jnp.bfloat16)

    return pl.pallas_call(
        body,
        out_shape=array(CH, ROWS, LANES),
        in_specs=[VMEM] * 8,
        scratch_shapes=[
            pltpu.VMEM((16, 2 * CH, LANES), jnp.bfloat16),
            pltpu.VMEM((12, 2 * CH, LANES), jnp.bfloat16),
            pltpu.VMEM((16, CH, LANES), jnp.bfloat16),
            pltpu.VMEM((16, CH, LANES), jnp.bfloat16),
            pltpu.VMEM((CH * ROWS, LANES), jnp.float32),
        ],
        compiler_params=SMALL,
        name="merge_rest",
    )(near_side, far_side, one, three, mine, *tables)


def on_device(frames, w_pair, w_mixed, slope_pair, slope_mixed):
    count = lax.axis_size("frame")
    quarter = count // 4
    rows = lax.axis_size("row")

    def swapped(block, mask):
        return lax.ppermute(block, "frame", [(i, i ^ (mask * quarter)) for i in range(count)])

    def on_chip(block):
        return lax.ppermute(block, "row", [(i, i ^ 1) for i in range(rows)])

    def off_chip(block):
        return lax.ppermute(block, "row", [(i, ((i + 1) ^ 1) - 1) for i in range(1, rows - 1)])

    own, one, three, two = spread(frames)
    one = swapped(one, 1)
    three = swapped(three, 3)
    two = swapped(two, 2)
    tables = weights(w_pair, w_mixed, slope_pair, slope_mixed)
    near_early, far_early = edges(own, two)
    far_early = off_chip(far_early)
    near_early = on_chip(near_early)
    near_late, far_late = edges(one, three)
    far_late = off_chip(far_late)
    near_late = on_chip(near_late)
    mine = merge_own(near_early, far_early, own, two, tables)
    merged = merge_rest(near_late, far_late, one, three, mine, tables)
    return merged[None]


def solution(mesh):
    placed = (P("frame", None, "row", None), P(), P(), P(), P())
    return jax.shard_map(
        on_device,
        mesh=mesh,
        in_specs=placed,
        out_specs=P("frame", None, "row", None),
        check_vma=False,
    )
```

profile of v0, /device:TPU:57, one launch (start us, length us, event | category | flops | bytes accessed | tf_op | source)
XLA Modules:
  0.0 41.9 jit_solution(15951648595660420347)
XLA Ops:
  0.0 0.0 copy-start
  0.0 1.0 %copy-done = bf16[4,64,8,128]{3,2,1,0:T(8,128)(2,1)S(1)} copy-done((bf16[4,64,8,128]{3,2,1,0:T(8,128)(2,1)S(1)}, bf16[4,64,8,128]{3,2,1,0:T(8,128)(2,1)}, u32[]{:S(2)}) %copy-start) | copy-done | bytes 524312
  1.0 0.2 spread.1
  1.3 10.6 %collective-permute-start.4 = (bf16[8,64,128]{2,1,0:T(8,128)(2,1)S(1)}, bf16[8,64,128]{2,1,0:T(8,128)(2,1)S(1)}, u32[]{:S(2)}, u32[]{:S(2)}) collective-permute-start(bf16[8,64,128]{2,1,0:T(8,128)(2,1)S(1)} %get-tuple-element.21), channel_id=1, source_target_pairs={{0,8},{1,9},{2,10},{3,11},{4,12},{5,13},{6,14},{7,15},{8,0},{9,1},... | collective-permute-start | bytes 393224 | tf_op jit(solution)/shard_map/ppermute | solution.py:202
  11.9 4.0 %collective-permute-start = (bf16[8,64,128]{2,1,0:T(8,128)(2,1)S(1)}, bf16[8,64,128]{2,1,0:T(8,128)(2,1)S(1)}, u32[]{:S(2)}, u32[]{:S(2)}) collective-permute-start(bf16[8,64,128]{2,1,0:T(8,128)(2,1)S(1)} %get-tuple-element.16), channel_id=1, source_target_pairs={{0,4},{1,5},{2,6},{3,7},{4,0},{5,1},{6,2},{7,3},{8,12},{9,13},{10,... | collective-permute-start | bytes 393224 | tf_op jit(solution)/shard_map/ppermute | solution.py:202
  15.9 1.9 %collective-permute-start.1 = (bf16[8,64,128]{2,1,0:T(8,128)(2,1)S(1)}, bf16[8,64,128]{2,1,0:T(8,128)(2,1)S(1)}, u32[]{:S(2)}, u32[]{:S(2)}) collective-permute-start(bf16[8,64,128]{2,1,0:T(8,128)(2,1)S(1)} %get-tuple-element.17), channel_id=1, source_target_pairs={{0,12},{1,13},{2,14},{3,15},{4,8},{5,9},{6,10},{7,11},{8,4},{9,5},... | collective-permute-start | bytes 393224 | tf_op jit(solution)/shard_map/ppermute | solution.py:202
  17.9 0.0 collective-permute-done.4.refs_1_.two_r
  17.9 0.0 copy-start.2
  17.9 0.0 copy-start.1
  17.9 3.3 %collective-permute-start.5 = (bf16[4,128,128]{2,1,0:T(8,128)(2,1)S(1)}, bf16[4,128,128]{2,1,0:T(8,128)(2,1)S(1)}, u32[]{:S(2)}, u32[]{:S(2)}) collective-permute-start(bf16[4,128,128]{2,1,0:T(8,128)(2,1)S(1)} %get-tuple-element.22), channel_id=1, source_target_pairs={{0,16},{16,0},{32,48},{48,32},{64,80},{80,64},{96,112},{112,96},{1... | collective-permute-start | bytes 393224 | tf_op jit(solution)/shard_map/ppermute | solution.py:205
  21.2 3.8 %collective-permute-start.6 = (bf16[4,128,128]{2,1,0:T(8,128)(2,1)S(1)}, bf16[4,128,128]{2,1,0:T(8,128)(2,1)S(1)}, u32[]{:S(2)}, u32[]{:S(2)}) collective-permute-start(bf16[4,128,128]{2,1,0:T(8,128)(2,1)S(1)} %get-tuple-element.23), channel_id=1, source_target_pairs={{16,32},{32,16},{48,64},{64,48},{80,96},{96,80},{112,128},{128,112... | collective-permute-start | bytes 393224 | tf_op jit(solution)/shard_map/ppermute | solution.py:208
  25.0 0.5 %collective-permute-done.refs_0_.one_r = bf16[8,64,128]{2,1,0:T(8,128)(2,1)S(1)} collective-permute-done((bf16[8,64,128]{2,1,0:T(8,128)(2,1)S(1)}, bf16[8,64,128]{2,1,0:T(8,128)(2,1)S(1)}, u32[]{:S(2)}, u32[]{:S(2)}) %collective-permute-start) | collective-permute-done | bytes 131104 | tf_op jit(solution)/shard_map/ppermute | solution.py:202
  25.4 0.6 %collective-permute-done.1.refs_1_.three_r = bf16[8,64,128]{2,1,0:T(8,128)(2,1)S(1)} collective-permute-done((bf16[8,64,128]{2,1,0:T(8,128)(2,1)S(1)}, bf16[8,64,128]{2,1,0:T(8,128)(2,1)S(1)}, u32[]{:S(2)}, u32[]{:S(2)}) %collective-permute-start.1) | collective-permute-done | bytes 131104 | tf_op jit(solution)/shard_map/ppermute | solution.py:202
  26.1 3.6 %collective-permute-start.2 = (bf16[4,128,128]{2,1,0:T(8,128)(2,1)S(1)}, bf16[4,128,128]{2,1,0:T(8,128)(2,1)S(1)}, u32[]{:S(2)}, u32[]{:S(2)}) collective-permute-start(bf16[4,128,128]{2,1,0:T(8,128)(2,1)S(1)} %get-tuple-element.18), channel_id=1, source_target_pairs={{0,16},{16,0},{32,48},{48,32},{64,80},{80,64},{96,112},{112,96},{1... | collective-permute-start | bytes 393224 | tf_op jit(solution)/shard_map/ppermute | solution.py:205
  29.7 3.8 %collective-permute-start.3 = (bf16[4,128,128]{2,1,0:T(8,128)(2,1)S(1)}, bf16[4,128,128]{2,1,0:T(8,128)(2,1)S(1)}, u32[]{:S(2)}, u32[]{:S(2)}) collective-permute-start(bf16[4,128,128]{2,1,0:T(8,128)(2,1)S(1)} %get-tuple-element.19), channel_id=1, source_target_pairs={{16,32},{32,16},{48,64},{64,48},{80,96},{96,80},{112,128},{128,112... | collective-permute-start | bytes 393224 | tf_op jit(solution)/shard_map/ppermute | solution.py:208
  33.4 0.0 copy-start.3
  33.5 0.0 copy-start.4
  33.5 0.0 copy-done.2
  33.5 0.0 copy-done.1
  33.5 0.6 %copy-done.3 = f32[64]{0:T(128)S(1)} copy-done((f32[64]{0:T(128)S(1)}, f32[64]{0:T(128)}, u32[]{:S(2)}) %copy-start.3) | copy-done | bytes 280
  34.1 0.0 copy-done.4
  34.1 0.2 weights.1
  34.3 0.0 collective-permute-done.5.near_r
  34.3 0.0 collective-permute-done.6.far_r
  34.3 1.0 %merge_own.1.mine_r = bf16[12,64,128]{2,1,0:T(8,128)(2,1)S(1)} custom-call(bf16[4,128,128]{2,1,0:T(8,128)(2,1)S(1)} %collective-permute-done.5.near_r, bf16[4,128,128]{2,1,0:T(8,128)(2,1)S(1)} %collective-permute-done.6.far_r, bf16[8,64,128]{2,1,0:T(8,128)(2,1)S(1)} %get-tuple-element.20.refs_0_.own_r, ...), custom_call_target="tpu_custom_call" | custom-call | tf_op jit(solution)/shard_map/merge_own/pallas_call | solution.py:148
  35.3 0.0 collective-permute-done.2.near_r
  35.3 4.3 %collective-permute-done.3.far_r = bf16[4,128,128]{2,1,0:T(8,128)(2,1)S(1)} collective-permute-done((bf16[4,128,128]{2,1,0:T(8,128)(2,1)S(1)}, bf16[4,128,128]{2,1,0:T(8,128)(2,1)S(1)}, u32[]{:S(2)}, u32[]{:S(2)}) %collective-permute-start.3) | collective-permute-done | bytes 131104 | tf_op jit(solution)/shard_map/ppermute | solution.py:208
  39.6 2.3 %merge_rest.1 = bf16[64,8,128]{2,1,0:T(8,128)(2,1)} custom-call(bf16[4,128,128]{2,1,0:T(8,128)(2,1)S(1)} %collective-permute-done.2.near_r, bf16[4,128,128]{2,1,0:T(8,128)(2,1)S(1)} %collective-permute-done.3.far_r, bf16[8,64,128]{2,1,0:T(8,128)(2,1)S(1)} %collective-permute-done.refs_0_.one_r, ...), custom_call_target="tpu_custom_call" | custom-call | tf_op jit(solution)/shard_map/merge_rest/pallas_call | solution.py:180
  (2 shorter events, 0.1 us)
Async XLA Ops:
  0.0 1.0 %copy-start = (bf16[4,64,8,128]{3,2,1,0:T(8,128)(2,1)S(1)}, bf16[4,64,8,128]{3,2,1,0:T(8,128)(2,1)}, u32[]{:S(2)}) copy-start(bf16[4,64,8,128]{3,2,1,0:T(8,128)(2,1)} %src.1) | copy-start | bytes 1572868
  1.3 16.6 %collective-permute-start.4 = (bf16[8,64,128]{2,1,0:T(8,128)(2,1)S(1)}, bf16[8,64,128]{2,1,0:T(8,128)(2,1)S(1)}, u32[]{:S(2)}, u32[]{:S(2)}) collective-permute-start(bf16[8,64,128]{2,1,0:T(8,128)(2,1)S(1)} %get-tuple-element.21), channel_id=1, source_target_pairs={{0,8},{1,9},{2,10},{3,11},{4,12},{5,13},{6,14},{7,15},{8,0},{9,1},... | collective-permute-start | bytes 393224 | tf_op jit(solution)/shard_map/ppermute | solution.py:202
  11.9 13.5 %collective-permute-start = (bf16[8,64,128]{2,1,0:T(8,128)(2,1)S(1)}, bf16[8,64,128]{2,1,0:T(8,128)(2,1)S(1)}, u32[]{:S(2)}, u32[]{:S(2)}) collective-permute-start(bf16[8,64,128]{2,1,0:T(8,128)(2,1)S(1)} %get-tuple-element.16), channel_id=1, source_target_pairs={{0,4},{1,5},{2,6},{3,7},{4,0},{5,1},{6,2},{7,3},{8,12},{9,13},{10,... | collective-permute-start | bytes 393224 | tf_op jit(solution)/shard_map/ppermute | solution.py:202
  15.9 10.1 %collective-permute-start.1 = (bf16[8,64,128]{2,1,0:T(8,128)(2,1)S(1)}, bf16[8,64,128]{2,1,0:T(8,128)(2,1)S(1)}, u32[]{:S(2)}, u32[]{:S(2)}) collective-permute-start(bf16[8,64,128]{2,1,0:T(8,128)(2,1)S(1)} %get-tuple-element.17), channel_id=1, source_target_pairs={{0,12},{1,13},{2,14},{3,15},{4,8},{5,9},{6,10},{7,11},{8,4},{9,5},... | collective-permute-start | bytes 393224 | tf_op jit(solution)/shard_map/ppermute | solution.py:202
  17.9 15.6 %copy-start.2 = (bf16[3,3,64,64]{3,2,1,0:T(8,128)(2,1)S(1)}, bf16[3,3,64,64]{3,2,1,0:T(8,128)(2,1)}, u32[]{:S(2)}) copy-start(bf16[3,3,64,64]{3,2,1,0:T(8,128)(2,1)} %param.7) | copy-start | bytes 221188
  17.9 15.6 %copy-start.1 = (bf16[3,3,64,128]{3,2,1,0:T(8,128)(2,1)S(1)}, bf16[3,3,64,128]{3,2,1,0:T(8,128)(2,1)}, u32[]{:S(2)}) copy-start(bf16[3,3,64,128]{3,2,1,0:T(8,128)(2,1)} %param.6) | copy-start | bytes 442372
  17.9 16.3 %collective-permute-start.5 = (bf16[4,128,128]{2,1,0:T(8,128)(2,1)S(1)}, bf16[4,128,128]{2,1,0:T(8,128)(2,1)S(1)}, u32[]{:S(2)}, u32[]{:S(2)}) collective-permute-start(bf16[4,128,128]{2,1,0:T(8,128)(2,1)S(1)} %get-tuple-element.22), channel_id=1, source_target_pairs={{0,16},{16,0},{32,48},{48,32},{64,80},{80,64},{96,112},{112,96},{1... | collective-permute-start | bytes 393224 | tf_op jit(solution)/shard_map/ppermute | solution.py:205
  21.2 13.1 %collective-permute-start.6 = (bf16[4,128,128]{2,1,0:T(8,128)(2,1)S(1)}, bf16[4,128,128]{2,1,0:T(8,128)(2,1)S(1)}, u32[]{:S(2)}, u32[]{:S(2)}) collective-permute-start(bf16[4,128,128]{2,1,0:T(8,128)(2,1)S(1)} %get-tuple-element.23), channel_id=1, source_target_pairs={{16,32},{32,16},{48,64},{64,48},{80,96},{96,80},{112,128},{128,112... | collective-permute-start | bytes 393224 | tf_op jit(solution)/shard_map/ppermute | solution.py:208
  26.1 9.2 %collective-permute-start.2 = (bf16[4,128,128]{2,1,0:T(8,128)(2,1)S(1)}, bf16[4,128,128]{2,1,0:T(8,128)(2,1)S(1)}, u32[]{:S(2)}, u32[]{:S(2)}) collective-permute-start(bf16[4,128,128]{2,1,0:T(8,128)(2,1)S(1)} %get-tuple-element.18), channel_id=1, source_target_pairs={{0,16},{16,0},{32,48},{48,32},{64,80},{80,64},{96,112},{112,96},{1... | collective-permute-start | bytes 393224 | tf_op jit(solution)/shard_map/ppermute | solution.py:205
  29.7 9.9 %collective-permute-start.3 = (bf16[4,128,128]{2,1,0:T(8,128)(2,1)S(1)}, bf16[4,128,128]{2,1,0:T(8,128)(2,1)S(1)}, u32[]{:S(2)}, u32[]{:S(2)}) collective-permute-start(bf16[4,128,128]{2,1,0:T(8,128)(2,1)S(1)} %get-tuple-element.19), channel_id=1, source_target_pairs={{16,32},{32,16},{48,64},{64,48},{80,96},{96,80},{112,128},{128,112... | collective-permute-start | bytes 393224 | tf_op jit(solution)/shard_map/ppermute | solution.py:208
  33.4 0.7 %copy-start.3 = (f32[64]{0:T(128)S(1)}, f32[64]{0:T(128)}, u32[]{:S(2)}) copy-start(f32[64]{0:T(128)} %param.8) | copy-start | bytes 772
  33.5 0.7 %copy-start.4 = (f32[64]{0:T(128)S(1)}, f32[64]{0:T(128)}, u32[]{:S(2)}) copy-start(f32[64]{0:T(128)} %param.9) | copy-start | bytes 772
where the time goes:
time: 42.3 us; the launch traced here: 41.9 us
  starting transfers between devices  30.9 us (73%)
  waiting for transfers between devices  5.34 us (13%)
  Pallas kernels  3.78 us (9%)
  local copies, waits for them, and re-layouts  1.69 us (4%)
    ppermute x3, starting transfers between devices, swapped(): lax.ppermute(block, 'frame', [(i, i ^ mask * quarter) for i in range(coun...  16.6 us
    ppermute x2, starting transfers between devices, off_chip(): lax.ppermute(block, 'row', [(i, (i + 1 ^ 1) - 1) for i in range(1, rows -...  7.51 us
    ppermute x2, starting transfers between devices, on_chip(): return lax.ppermute(block, 'row', [(i, i ^ 1) for i in range(rows)])  6.87 us
    ppermute x2, waiting for transfers between devices, off_chip(): lax.ppermute(block, 'row', [(i, (i + 1 ^ 1) - 1) for i in range(1, rows -...  4.26 us
    pallas_call x1, Pallas kernels, merge_rest(): pl.pallas_call(body, out_shape=array(CH, ROWS, LANES), in_specs=[VMEM] *...  2.34 us
    unnamed x10, local copies, waits for them, and re-layouts  1.69 us
    ppermute x3, waiting for transfers between devices, swapped(): lax.ppermute(block, 'frame', [(i, i ^ mask * quarter) for i in range(coun...  1.07 us
    pallas_call x1, Pallas kernels, merge_own(): pl.pallas_call(body, out_shape=array(12, CH, LANES), in_specs=[VMEM] * 7,...  1 us
  transfers between devices with their start and end apart: 7, of which 3 were waited for; matrix products, arithmetic and copies ran while one was open for 0% of the time, Pallas kernels for 3%

commit v1 on v0

v1 whole, which is shorter than its diff:
```python
import jax
import jax.numpy as jnp
from jax import lax
from jax.experimental import pallas as pl
from jax.experimental.pallas import tpu as pltpu
from jax.sharding import PartitionSpec as P


ROWS = 8
HALO = 4
CH = 64
LANES = 128
VMEM = pl.BlockSpec(memory_space=pltpu.VMEM)
SMALL = pltpu.CompilerParams(vmem_limit_bytes=8 << 20)


def array(*shape, dtype=jnp.bfloat16):
    return jax.ShapeDtypeStruct(shape, dtype)


def position():
    return lax.axis_index("frame") // (lax.axis_size("frame") // 4)


def odd_row():
    return lax.axis_index("row") % 2


def spread(frames):
    def body(src, own, one, three, two, wide):
        at = position()
        turn = 7 - 7 * odd_row()
        sign = 2 * odd_row() - 1
        for k, out in ((2, two), (1, one), (3, three), (0, own)):
            wide[k] = src[at ^ k].astype(jnp.float32).reshape(CH * ROWS, LANES)
            for row in range(ROWS):
                out[turn + sign * row] = wide[k, pl.ds(row, CH, stride=ROWS), :].astype(jnp.bfloat16)

    return pl.pallas_call(
        body,
        out_shape=(array(ROWS, CH, LANES),) * 4,
        in_specs=[VMEM],
        out_specs=(VMEM,) * 4,
        scratch_shapes=[pltpu.VMEM((4, CH * ROWS, LANES), jnp.float32)],
        compiler_params=SMALL,
        name="spread",
    )(frames)


def weights(w_pair, w_mixed, slope_pair, slope_mixed):
    def body(wp, wm, sp, sm, pair, mixed, cols):
        top = 2 - 2 * odd_row()
        taps = (top, 1, 2 - top)
        for ky in range(3):
            at = ky * 2 * CH
            tap = wp[taps[ky]]
            pair[0, :, at : at + 2 * CH] = tap
            pair[1, :, at : at + 2 * CH] = jnp.concatenate([tap[:, CH:], tap[:, :CH]], axis=1)
        mixed[...] = jnp.concatenate([wm[taps[0]], wm[1], wm[taps[2]]], axis=1)
        square = lax.broadcasted_iota(jnp.int32, (CH, CH), 0) == lax.broadcasted_iota(jnp.int32, (CH, CH), 1)
        for k, slope in enumerate((sp, sm)):
            column = jnp.sum(jnp.where(square, slope[...], 0.0), axis=1, keepdims=True)
            cols[k] = jnp.broadcast_to(column, (CH, LANES))

    return pl.pallas_call(
        body,
        out_shape=(array(2, 3 * CH, 6 * CH), array(3 * CH, 3 * CH), array(2, CH, LANES, dtype=jnp.float32)),
        in_specs=[VMEM] * 4,
        out_specs=(VMEM,) * 3,
        compiler_params=SMALL,
        name="weights",
    )(w_pair.reshape(3, 3 * CH, 2 * CH), w_mixed.reshape(3, 3 * CH, CH), slope_pair.reshape(1, CH), slope_mixed.reshape(1, CH))


def edges(*frames):
    def body(*refs):
        near_side, far_side = refs[-2:]
        for k, frame in enumerate(refs[:-2]):
            for row in range(HALO):
                near_side[row, k * CH : (k + 1) * CH, :] = frame[HALO - 1 - row]
                far_side[row, k * CH : (k + 1) * CH, :] = frame[ROWS - 1 - row]

    half = array(HALO, len(frames) * CH, LANES)
    return pl.pallas_call(
        body,
        out_shape=(half, half),
        in_specs=[VMEM] * len(frames),
        out_specs=(VMEM,) * 2,
        compiler_params=SMALL,
        name="edges",
    )(*frames)


def fill(stack, slot, source, at, part=0):
    to = slice(slot * CH, (slot + 1) * CH)
    stack[at : at + source.shape[0], to, :] = source[:, part * CH : (part + 1) * CH, :]


class Level:
    def __init__(self, pair, mixed, cols, swap, hid):
        lane = lax.broadcasted_iota(jnp.int32, (CH, LANES), 1)
        self.not_first = lane > 0
        self.not_last = lane < LANES - 1
        self.pair = pair[swap]
        self.mixed = mixed[...]
        self.cols = cols
        self.swap = swap
        self.hid = hid
        place = lax.axis_index("row")
        self.edge = (place == 0) | (place == lax.axis_size("row") - 1)

    def inside(self, row, value):
        return jnp.where(self.edge, 0.0, value) if row >= HALO + ROWS else value

    def fold(self, part, which):
        left = jnp.where(self.not_first, pltpu.roll(part[:CH], 1, 1), 0.0)
        right = jnp.where(self.not_last, pltpu.roll(part[2 * CH :], LANES - 1, 1), 0.0)
        total = part[CH : 2 * CH] + left + right
        return jnp.maximum(total, self.cols[which] * total)

    def product(self, lhs, stack, row, depth):
        rhs = jnp.concatenate([stack[r - 1 : r + 2].reshape(3 * depth, LANES) for r in (row, row + 1)], axis=1)
        return jnp.dot(lhs, rhs, preferred_element_type=jnp.float32)

    def first(self, stack, shift, low, high):
        for row in range(low, high, 2):
            both = self.product(self.pair, stack, row - shift, 2 * CH)
            for k in range(2):
                value = self.fold(both[:, k * LANES : (k + 1) * LANES], 0)
                self.hid[row + k] = self.inside(row + k, value).astype(jnp.bfloat16)

    def second(self, stack, shift, low, high, emit):
        for row in range(low, high, 2):
            both = self.product(self.mixed, self.hid, row, CH)
            for k in range(2):
                start = stack[row + k - shift, pl.ds(self.swap * CH, CH), :].astype(jnp.float32)
                branch = self.fold(both[:, k * LANES : (k + 1) * LANES], 1)
                emit(row + k, self.inside(row + k, start + branch))


def into(target, shift, to):
    def emit(row, value):
        target[row - shift, to, :] = value.astype(target.dtype)

    return emit


OTHER = slice(CH, 2 * CH)
HIDDEN = pltpu.VMEM((16, CH, LANES), jnp.bfloat16)
STACK = pltpu.VMEM((16, 2 * CH, LANES), jnp.bfloat16)


def merge_own(near_side, far_side, own, two, tables):
    def body(near_r, far_r, own_r, two_r, pair, mixed, cols, out, stack, hid):
        for slot, frame in enumerate((own_r, two_r)):
            fill(stack, slot, near_r, 0, slot)
            fill(stack, slot, frame, HALO)
            fill(stack, slot, far_r, HALO + ROWS, slot)
        level = Level(pair, mixed, cols, position() // 2, hid)
        level.first(stack, 0, 1, 15)
        level.second(stack, 0, 2, 14, into(out, 2, slice(None)))

    return pl.pallas_call(
        body,
        out_shape=array(12, CH, LANES),
        in_specs=[VMEM] * 7,
        out_specs=VMEM,
        scratch_shapes=[STACK, HIDDEN],
        compiler_params=SMALL,
        name="merge_own",
    )(near_side, far_side, own, two, *tables)


def merge_inner(near_side, one, three, mine, tables):
    def body(near_r, one_r, three_r, mine_r, pair, mixed, cols, hid_end, ones_end, top_end, done, stack, ones, hid, top_hid):
        for slot, frame in enumerate((one_r, three_r)):
            fill(stack, slot, near_r, 0, slot)
            fill(stack, slot, frame, HALO)
        fill(ones, 0, mine_r.at[0:8], 2)
        at = position()
        level = Level(pair, mixed, cols, at // 2, hid)
        level.first(stack, 0, 1, 11)
        level.second(stack, 0, 2, 10, into(ones, 0, OTHER))
        top = Level(pair, mixed, cols, at % 2, top_hid)
        top.first(ones, 0, 3, 9)
        top.second(ones, 0, 4, 8, into(done, 4, slice(None)))
        hid_end[...] = hid[9:11]
        ones_end[...] = ones[8:10]
        top_end[...] = top_hid[7:9]

    return pl.pallas_call(
        body,
        out_shape=(array(2, CH, LANES), array(2, 2 * CH, LANES), array(2, CH, LANES), array(4, CH, LANES, dtype=jnp.float32)),
        in_specs=[VMEM] * 7,
        out_specs=(VMEM,) * 4,
        scratch_shapes=[STACK, STACK, HIDDEN, HIDDEN],
        compiler_params=SMALL,
        name="merge_inner",
    )(near_side, one, three, mine, *tables)


def merge_outer(far_side, one, three, mine, inner, tables):
    def body(far_r, one_r, three_r, mine_r, hid_end, ones_end, top_end, done, pair, mixed, cols, out, stack, ones, hid, top_hid, rows, wide):
        for slot, frame in enumerate((one_r, three_r)):
            fill(stack, slot, frame.at[6:8], 10)
            fill(stack, slot, far_r, HALO + ROWS, slot)
        hid[9:11] = hid_end[...]
        ones[8:10] = ones_end[...]
        fill(ones, 0, mine_r.at[8:12], 10)
        top_hid[7:9] = top_end[...]
        rows[0:4] = done[...]
        at = position()
        level = Level(pair, mixed, cols, at // 2, hid)
        level.first(stack, 0, 11, 15)
        level.second(stack, 0, 10, 14, into(ones, 0, OTHER))
        top = Level(pair, mixed, cols, at % 2, top_hid)
        top.first(ones, 0, 9, 13)
        top.second(ones, 0, 8, 12, into(rows, 4, slice(None)))
        turn = 7 - 7 * odd_row()
        sign = 2 * odd_row() - 1
        for row in range(ROWS):
            wide[pl.ds(row, CH, stride=ROWS), :] = rows[turn + sign * row]
        out[...] = wide[...].reshape(CH, ROWS, LANES).astype(jnp.bfloat16)

    return pl.pallas_call(
        body,
        out_shape=array(CH, ROWS, LANES),
        in_specs=[VMEM] * 11,
        scratch_shapes=[
            STACK,
            STACK,
            HIDDEN,
            HIDDEN,
            pltpu.VMEM((ROWS, CH, LANES), jnp.float32),
            pltpu.VMEM((CH * ROWS, LANES), jnp.float32),
        ],
        compiler_params=SMALL,
        name="merge_outer",
    )(far_side, one, three, mine, *inner, *tables)


def on_device(frames, w_pair, w_mixed, slope_pair, slope_mixed):
    count = lax.axis_size("frame")
    quarter = count // 4
    rows = lax.axis_size("row")

    def swapped(block, mask):
        return lax.ppermute(block, "frame", [(i, i ^ (mask * quarter)) for i in range(count)])

    def on_chip(block):
        return lax.ppermute(block, "row", [(i, i ^ 1) for i in range(rows)])

    def off_chip(block):
        return lax.ppermute(block, "row", [(i, ((i + 1) ^ 1) - 1) for i in range(1, rows - 1)])

    own, one, three, two = spread(frames)
    one = swapped(one, 1)
    three = swapped(three, 3)
    two = swapped(two, 2)
    tables = weights(w_pair, w_mixed, slope_pair, slope_mixed)
    near_early, far_early = edges(own, two)
    far_early = off_chip(far_early)
    near_early = on_chip(near_early)
    near_late, far_late = edges(one, three)
    far_late = off_chip(far_late)
    near_late = on_chip(near_late)
    mine = merge_own(near_early, far_early, own, two, tables)
    inner = merge_inner(near_late, one, three, mine, tables)
    merged = merge_outer(far_late, one, three, mine, inner, tables)
    return merged[None]


def solution(mesh):
    placed = (P("frame", None, "row", None), P(), P(), P(), P())
    return jax.shard_map(
        on_device,
        mesh=mesh,
        in_specs=placed,
        out_specs=P("frame", None, "row", None),
        check_vma=False,
    )
```

time: 42.3 us -> 41.9 us (level)
  waiting for transfers between devices: 5.34 us -> 3.89 us
  Pallas kernels: 3.78 us -> 4.84 us
    ppermute x2, waiting for transfers between devices: 4.26 us -> 2.8 us  [off_chip(): lax.ppermute(block, 'row', [(i, (i + 1 ^ 1) - 1) for i in range(1, rows -...]
    pallas_call x1 -> x2, Pallas kernels: 2.34 us -> 3.43 us  [the longest x1 1.95 us: merge_outer(): pl.pallas_call(body, out_shape=array(CH, ROWS, LANES), in_specs=[VMEM] *...]
  transfers between devices with their start and end apart: 7 -> 7, of which waited for: 3 -> 3; matrix products, arithmetic and copies ran while one was open for 0% -> 0% of each run, Pallas kernels for 3% -> 6%
where the time goes in v1:
time: 41.9 us; the launch traced here: 41.5 us
  starting transfers between devices  30.9 us (74%)
  Pallas kernels  4.84 us (12%)
  waiting for transfers between devices  3.89 us (9%)
  local copies, waits for them, and re-layouts  1.69 us (4%)
    ppermute x3, starting transfers between devices, swapped(): lax.ppermute(block, 'frame', [(i, i ^ mask * quarter) for i in range(coun...  16.6 us
    ppermute x2, starting transfers between devices, off_chip(): lax.ppermute(block, 'row', [(i, (i + 1 ^ 1) - 1) for i in range(1, rows -...  7.51 us
    ppermute x2, starting transfers between devices, on_chip(): return lax.ppermute(block, 'row', [(i, i ^ 1) for i in range(rows)])  6.87 us
    ppermute x2, waiting for transfers between devices, off_chip(): lax.ppermute(block, 'row', [(i, (i + 1 ^ 1) - 1) for i in range(1, rows -...  2.8 us
    pallas_call x1, Pallas kernels, merge_outer(): pl.pallas_call(body, out_shape=array(CH, ROWS, LANES), in_specs=[VMEM] *...  1.95 us
    unnamed x10, local copies, waits for them, and re-layouts  1.69 us
    pallas_call x1, Pallas kernels, merge_inner(): pl.pallas_call(body, out_shape=(array(2, CH, LANES), array(2, 2 * CH, LAN...  1.47 us
    ppermute x3, waiting for transfers between devices, swapped(): lax.ppermute(block, 'frame', [(i, i ^ mask * quarter) for i in range(coun...  1.09 us
  transfers between devices with their start and end apart: 7, of which 3 were waited for; matrix products, arithmetic and copies ran while one was open for 0% of the time, Pallas kernels for 6%

profile of v1, /device:TPU:57, one launch (start us, length us, event | category | flops | bytes accessed | tf_op | source)
XLA Modules:
  0.0 41.5 jit_solution(6464725311277785969)
XLA Ops:
  0.0 0.0 copy-start
  0.0 1.0 %copy-done = bf16[4,64,8,128]{3,2,1,0:T(8,128)(2,1)S(1)} copy-done((bf16[4,64,8,128]{3,2,1,0:T(8,128)(2,1)S(1)}, bf16[4,64,8,128]{3,2,1,0:T(8,128)(2,1)}, u32[]{:S(2)}) %copy-start) | copy-done | bytes 524312
  1.0 0.2 spread.1
  1.3 10.6 %collective-permute-start.3 = (bf16[8,64,128]{2,1,0:T(8,128)(2,1)S(1)}, bf16[8,64,128]{2,1,0:T(8,128)(2,1)S(1)}, u32[]{:S(2)}, u32[]{:S(2)}) collective-permute-start(bf16[8,64,128]{2,1,0:T(8,128)(2,1)S(1)} %get-tuple-element.24), channel_id=1, source_target_pairs={{0,8},{1,9},{2,10},{3,11},{4,12},{5,13},{6,14},{7,15},{8,0},{9,1},... | collective-permute-start | bytes 393224 | tf_op jit(solution)/shard_map/ppermute | solution.py:248
  11.9 4.0 %collective-permute-start = (bf16[8,64,128]{2,1,0:T(8,128)(2,1)S(1)}, bf16[8,64,128]{2,1,0:T(8,128)(2,1)S(1)}, u32[]{:S(2)}, u32[]{:S(2)}) collective-permute-start(bf16[8,64,128]{2,1,0:T(8,128)(2,1)S(1)} %get-tuple-element.20), channel_id=1, source_target_pairs={{0,4},{1,5},{2,6},{3,7},{4,0},{5,1},{6,2},{7,3},{8,12},{9,13},{10,... | collective-permute-start | bytes 393224 | tf_op jit(solution)/shard_map/ppermute | solution.py:248
  15.9 1.9 %collective-permute-start.1 = (bf16[8,64,128]{2,1,0:T(8,128)(2,1)S(1)}, bf16[8,64,128]{2,1,0:T(8,128)(2,1)S(1)}, u32[]{:S(2)}, u32[]{:S(2)}) collective-permute-start(bf16[8,64,128]{2,1,0:T(8,128)(2,1)S(1)} %get-tuple-element.21), channel_id=1, source_target_pairs={{0,12},{1,13},{2,14},{3,15},{4,8},{5,9},{6,10},{7,11},{8,4},{9,5},... | collective-permute-start | bytes 393224 | tf_op jit(solution)/shard_map/ppermute | solution.py:248
  17.9 0.0 collective-permute-done.3.refs_1_.two_r
  17.9 0.0 copy-start.2
  17.9 0.0 copy-start.1
  17.9 3.3 %collective-permute-start.4 = (bf16[4,128,128]{2,1,0:T(8,128)(2,1)S(1)}, bf16[4,128,128]{2,1,0:T(8,128)(2,1)S(1)}, u32[]{:S(2)}, u32[]{:S(2)}) collective-permute-start(bf16[4,128,128]{2,1,0:T(8,128)(2,1)S(1)} %get-tuple-element.25), channel_id=1, source_target_pairs={{0,16},{16,0},{32,48},{48,32},{64,80},{80,64},{96,112},{112,96},{1... | collective-permute-start | bytes 393224 | tf_op jit(solution)/shard_map/ppermute | solution.py:251
  21.2 3.8 %collective-permute-start.5 = (bf16[4,128,128]{2,1,0:T(8,128)(2,1)S(1)}, bf16[4,128,128]{2,1,0:T(8,128)(2,1)S(1)}, u32[]{:S(2)}, u32[]{:S(2)}) collective-permute-start(bf16[4,128,128]{2,1,0:T(8,128)(2,1)S(1)} %get-tuple-element.26), channel_id=1, source_target_pairs={{16,32},{32,16},{48,64},{64,48},{80,96},{96,80},{112,128},{128,112... | collective-permute-start | bytes 393224 | tf_op jit(solution)/shard_map/ppermute | solution.py:254
  25.0 0.5 %collective-permute-done.refs_0_.one_r = bf16[8,64,128]{2,1,0:T(8,128)(2,1)S(1)} collective-permute-done((bf16[8,64,128]{2,1,0:T(8,128)(2,1)S(1)}, bf16[8,64,128]{2,1,0:T(8,128)(2,1)S(1)}, u32[]{:S(2)}, u32[]{:S(2)}) %collective-permute-start) | collective-permute-done | bytes 131104 | tf_op jit(solution)/shard_map/ppermute | solution.py:248
  25.5 0.6 %collective-permute-done.1.refs_1_.three_r = bf16[8,64,128]{2,1,0:T(8,128)(2,1)S(1)} collective-permute-done((bf16[8,64,128]{2,1,0:T(8,128)(2,1)S(1)}, bf16[8,64,128]{2,1,0:T(8,128)(2,1)S(1)}, u32[]{:S(2)}, u32[]{:S(2)}) %collective-permute-start.1) | collective-permute-done | bytes 131104 | tf_op jit(solution)/shard_map/ppermute | solution.py:248
  26.1 3.6 %collective-permute-start.6 = (bf16[4,128,128]{2,1,0:T(8,128)(2,1)S(1)}, bf16[4,128,128]{2,1,0:T(8,128)(2,1)S(1)}, u32[]{:S(2)}, u32[]{:S(2)}) collective-permute-start(bf16[4,128,128]{2,1,0:T(8,128)(2,1)S(1)} %get-tuple-element.30), channel_id=1, source_target_pairs={{0,16},{16,0},{32,48},{48,32},{64,80},{80,64},{96,112},{112,96},{1... | collective-permute-start | bytes 393224 | tf_op jit(solution)/shard_map/ppermute | solution.py:251
  29.7 3.8 %collective-permute-start.2 = (bf16[4,128,128]{2,1,0:T(8,128)(2,1)S(1)}, bf16[4,128,128]{2,1,0:T(8,128)(2,1)S(1)}, u32[]{:S(2)}, u32[]{:S(2)}) collective-permute-start(bf16[4,128,128]{2,1,0:T(8,128)(2,1)S(1)} %get-tuple-element.22), channel_id=1, source_target_pairs={{16,32},{32,16},{48,64},{64,48},{80,96},{96,80},{112,128},{128,112... | collective-permute-start | bytes 393224 | tf_op jit(solution)/shard_map/ppermute | solution.py:254
  33.5 0.0 copy-start.3
  33.5 0.0 copy-start.4
  33.5 0.0 copy-done.2
  33.5 0.0 copy-done.1
  33.5 0.6 %copy-done.3 = f32[64]{0:T(128)S(1)} copy-done((f32[64]{0:T(128)S(1)}, f32[64]{0:T(128)}, u32[]{:S(2)}) %copy-start.3) | copy-done | bytes 280
  34.1 0.0 copy-done.4
  34.1 0.2 weights.1
  34.3 0.0 collective-permute-done.4.near_r
  34.3 0.0 collective-permute-done.5.far_r
  34.3 1.0 %merge_own.1.mine_r = bf16[12,64,128]{2,1,0:T(8,128)(2,1)S(1)} custom-call(bf16[4,128,128]{2,1,0:T(8,128)(2,1)S(1)} %collective-permute-done.4.near_r, bf16[4,128,128]{2,1,0:T(8,128)(2,1)S(1)} %collective-permute-done.5.far_r, bf16[8,64,128]{2,1,0:T(8,128)(2,1)S(1)} %get-tuple-element.23.refs_0_.own_r, ...), custom_call_target="tpu_custom_call" | custom-call | tf_op jit(solution)/shard_map/merge_own/pallas_call | solution.py:163
  35.3 0.0 collective-permute-done.6.near_r
  35.3 1.5 %merge_inner.1 = (bf16[2,64,128]{2,1,0:T(8,128)(2,1)S(1)}, bf16[2,128,128]{2,1,0:T(8,128)(2,1)S(1)}, bf16[2,64,128]{2,1,0:T(8,128)(2,1)S(1)}, f32[4,64,128]{2,1,0:T(8,128)S(1)}) custom-call(bf16[4,128,128]{2,1,0:T(8,128)(2,1)S(1)} %collective-permute-done.6.near_r, bf16[8,64,128]{2,1,0:T(8,128)(2,1)S(1)} %collective-permute-done.refs_0_.one_r, ...), custom_call_target="tpu_custom_call" | custom-call | tf_op jit(solution)/shard_map/merge_inner/pallas_call | solution.py:191
  36.8 2.8 %collective-permute-done.2.far_r = bf16[4,128,128]{2,1,0:T(8,128)(2,1)S(1)} collective-permute-done((bf16[4,128,128]{2,1,0:T(8,128)(2,1)S(1)}, bf16[4,128,128]{2,1,0:T(8,128)(2,1)S(1)}, u32[]{:S(2)}, u32[]{:S(2)}) %collective-permute-start.2) | collective-permute-done | bytes 131104 | tf_op jit(solution)/shard_map/ppermute | solution.py:254
  39.6 2.0 %merge_outer.1 = bf16[64,8,128]{2,1,0:T(8,128)(2,1)} custom-call(bf16[4,128,128]{2,1,0:T(8,128)(2,1)S(1)} %collective-permute-done.2.far_r, bf16[8,64,128]{2,1,0:T(8,128)(2,1)S(1)} %collective-permute-done.refs_0_.one_r, bf16[8,64,128]{2,1,0:T(8,128)(2,1)S(1)} %collective-permute-done.1.refs_1_.three_r, bf16[12,64,128]{2,1,0:T(8,128)(2,1)S(1)} %merge_own.1.mine_r, ...), custom_call_target="tpu_custom_call" | custom-call | tf_op jit(solution)/shard_map/merge_outer/pallas_call | solution.py:225
  (2 shorter events, 0.0 us)
Async XLA Ops:
  0.0 1.0 %copy-start = (bf16[4,64,8,128]{3,2,1,0:T(8,128)(2,1)S(1)}, bf16[4,64,8,128]{3,2,1,0:T(8,128)(2,1)}, u32[]{:S(2)}) copy-start(bf16[4,64,8,128]{3,2,1,0:T(8,128)(2,1)} %src.1) | copy-start | bytes 1572868
  1.3 16.6 %collective-permute-start.3 = (bf16[8,64,128]{2,1,0:T(8,128)(2,1)S(1)}, bf16[8,64,128]{2,1,0:T(8,128)(2,1)S(1)}, u32[]{:S(2)}, u32[]{:S(2)}) collective-permute-start(bf16[8,64,128]{2,1,0:T(8,128)(2,1)S(1)} %get-tuple-element.24), channel_id=1, source_target_pairs={{0,8},{1,9},{2,10},{3,11},{4,12},{5,13},{6,14},{7,15},{8,0},{9,1},... | collective-permute-start | bytes 393224 | tf_op jit(solution)/shard_map/ppermute | solution.py:248
  11.9 13.5 %collective-permute-start = (bf16[8,64,128]{2,1,0:T(8,128)(2,1)S(1)}, bf16[8,64,128]{2,1,0:T(8,128)(2,1)S(1)}, u32[]{:S(2)}, u32[]{:S(2)}) collective-permute-start(bf16[8,64,128]{2,1,0:T(8,128)(2,1)S(1)} %get-tuple-element.20), channel_id=1, source_target_pairs={{0,4},{1,5},{2,6},{3,7},{4,0},{5,1},{6,2},{7,3},{8,12},{9,13},{10,... | collective-permute-start | bytes 393224 | tf_op jit(solution)/shard_map/ppermute | solution.py:248
  15.9 10.1 %collective-permute-start.1 = (bf16[8,64,128]{2,1,0:T(8,128)(2,1)S(1)}, bf16[8,64,128]{2,1,0:T(8,128)(2,1)S(1)}, u32[]{:S(2)}, u32[]{:S(2)}) collective-permute-start(bf16[8,64,128]{2,1,0:T(8,128)(2,1)S(1)} %get-tuple-element.21), channel_id=1, source_target_pairs={{0,12},{1,13},{2,14},{3,15},{4,8},{5,9},{6,10},{7,11},{8,4},{9,5},... | collective-permute-start | bytes 393224 | tf_op jit(solution)/shard_map/ppermute | solution.py:248
  17.9 15.6 %copy-start.2 = (bf16[3,3,64,64]{3,2,1,0:T(8,128)(2,1)S(1)}, bf16[3,3,64,64]{3,2,1,0:T(8,128)(2,1)}, u32[]{:S(2)}) copy-start(bf16[3,3,64,64]{3,2,1,0:T(8,128)(2,1)} %param.7) | copy-start | bytes 221188
  17.9 15.6 %copy-start.1 = (bf16[3,3,64,128]{3,2,1,0:T(8,128)(2,1)S(1)}, bf16[3,3,64,128]{3,2,1,0:T(8,128)(2,1)}, u32[]{:S(2)}) copy-start(bf16[3,3,64,128]{3,2,1,0:T(8,128)(2,1)} %param.6) | copy-start | bytes 442372
  17.9 16.4 %collective-permute-start.4 = (bf16[4,128,128]{2,1,0:T(8,128)(2,1)S(1)}, bf16[4,128,128]{2,1,0:T(8,128)(2,1)S(1)}, u32[]{:S(2)}, u32[]{:S(2)}) collective-permute-start(bf16[4,128,128]{2,1,0:T(8,128)(2,1)S(1)} %get-tuple-element.25), channel_id=1, source_target_pairs={{0,16},{16,0},{32,48},{48,32},{64,80},{80,64},{96,112},{112,96},{1... | collective-permute-start | bytes 393224 | tf_op jit(solution)/shard_map/ppermute | solution.py:251
  21.2 13.1 %collective-permute-start.5 = (bf16[4,128,128]{2,1,0:T(8,128)(2,1)S(1)}, bf16[4,128,128]{2,1,0:T(8,128)(2,1)S(1)}, u32[]{:S(2)}, u32[]{:S(2)}) collective-permute-start(bf16[4,128,128]{2,1,0:T(8,128)(2,1)S(1)} %get-tuple-element.26), channel_id=1, source_target_pairs={{16,32},{32,16},{48,64},{64,48},{80,96},{96,80},{112,128},{128,112... | collective-permute-start | bytes 393224 | tf_op jit(solution)/shard_map/ppermute | solution.py:254
  26.1 9.2 %collective-permute-start.6 = (bf16[4,128,128]{2,1,0:T(8,128)(2,1)S(1)}, bf16[4,128,128]{2,1,0:T(8,128)(2,1)S(1)}, u32[]{:S(2)}, u32[]{:S(2)}) collective-permute-start(bf16[4,128,128]{2,1,0:T(8,128)(2,1)S(1)} %get-tuple-element.30), channel_id=1, source_target_pairs={{0,16},{16,0},{32,48},{48,32},{64,80},{80,64},{96,112},{112,96},{1... | collective-permute-start | bytes 393224 | tf_op jit(solution)/shard_map/ppermute | solution.py:251
  29.7 9.9 %collective-permute-start.2 = (bf16[4,128,128]{2,1,0:T(8,128)(2,1)S(1)}, bf16[4,128,128]{2,1,0:T(8,128)(2,1)S(1)}, u32[]{:S(2)}, u32[]{:S(2)}) collective-permute-start(bf16[4,128,128]{2,1,0:T(8,128)(2,1)S(1)} %get-tuple-element.22), channel_id=1, source_target_pairs={{16,32},{32,16},{48,64},{64,48},{80,96},{96,80},{112,128},{128,112... | collective-permute-start | bytes 393224 | tf_op jit(solution)/shard_map/ppermute | solution.py:254
  33.5 0.7 %copy-start.3 = (f32[64]{0:T(128)S(1)}, f32[64]{0:T(128)}, u32[]{:S(2)}) copy-start(f32[64]{0:T(128)} %param.8) | copy-start | bytes 772
  33.5 0.7 %copy-start.4 = (f32[64]{0:T(128)S(1)}, f32[64]{0:T(128)}, u32[]{:S(2)}) copy-start(f32[64]{0:T(128)} %param.9) | copy-start | bytes 772

commit v2 on v1

--- a/solution.py
+++ b/solution.py
@@ -10,6 +10,7 @@
 HALO = 4
 CH = 64
 LANES = 128
+PIECES = 4
 VMEM = pl.BlockSpec(memory_space=pltpu.VMEM)
 SMALL = pltpu.CompilerParams(vmem_limit_bytes=8 << 20)
 
@@ -200,7 +201,7 @@
 
 
 def merge_outer(far_side, one, three, mine, inner, tables):
-    def body(far_r, one_r, three_r, mine_r, hid_end, ones_end, top_end, done, pair, mixed, cols, out, stack, ones, hid, top_hid, rows, wide):
+    def body(far_r, one_r, three_r, mine_r, hid_end, ones_end, top_end, done, pair, mixed, cols, out, stack, ones, hid, top_hid, rows, wide, held, sems):
         for slot, frame in enumerate((one_r, three_r)):
             fill(stack, slot, frame.at[6:8], 10)
             fill(stack, slot, far_r, HALO + ROWS, slot)
@@ -220,12 +221,21 @@
         sign = 2 * odd_row() - 1
         for row in range(ROWS):
             wide[pl.ds(row, CH, stride=ROWS), :] = rows[turn + sign * row]
-        out[...] = wide[...].reshape(CH, ROWS, LANES).astype(jnp.bfloat16)
+        copies = []
+        for k in range(PIECES):
+            some = slice(k * CH // PIECES, (k + 1) * CH // PIECES)
+            part = wide[some.start * ROWS : some.stop * ROWS, :]
+            held[some] = part.reshape(CH // PIECES, ROWS, LANES).astype(jnp.bfloat16)
+            copies.append(pltpu.make_async_copy(held.at[some], out.at[some], sems.at[k]))
+            copies[k].start()
+        for copy in copies:
+            copy.wait()
 
     return pl.pallas_call(
         body,
         out_shape=array(CH, ROWS, LANES),
         in_specs=[VMEM] * 11,
+        out_specs=pl.BlockSpec(memory_space=pl.ANY),
         scratch_shapes=[
             STACK,
             STACK,
@@ -233,6 +243,8 @@
             HIDDEN,
             pltpu.VMEM((ROWS, CH, LANES), jnp.float32),
             pltpu.VMEM((CH * ROWS, LANES), jnp.float32),
+            pltpu.VMEM((CH, ROWS, LANES), jnp.bfloat16),
+            pltpu.SemaphoreType.DMA((PIECES,)),
         ],
         compiler_params=SMALL,
         name="merge_outer",

time: 41.9 us -> 41.9 us (level)
  no operation moved by 1% of the time
where the time goes in v2:
time: 41.9 us; the launch traced here: 41.5 us
  starting transfers between devices  30.9 us (74%)
  Pallas kernels  4.84 us (12%)
  waiting for transfers between devices  3.89 us (9%)
  local copies, waits for them, and re-layouts  1.69 us (4%)
    ppermute x3, starting transfers between devices, swapped(): lax.ppermute(block, 'frame', [(i, i ^ mask * quarter) for i in range(coun...  16.6 us
    ppermute x2, starting transfers between devices, off_chip(): lax.ppermute(block, 'row', [(i, (i + 1 ^ 1) - 1) for i in range(1, rows -...  7.51 us
    ppermute x2, starting transfers between devices, on_chip(): return lax.ppermute(block, 'row', [(i, i ^ 1) for i in range(rows)])  6.87 us
    ppermute x2, waiting for transfers between devices, off_chip(): lax.ppermute(block, 'row', [(i, (i + 1 ^ 1) - 1) for i in range(1, rows -...  2.8 us
    pallas_call x1, Pallas kernels, merge_outer(): pl.pallas_call(body, out_shape=array(CH, ROWS, LANES), in_specs=[VMEM] *...  1.95 us
    unnamed x10, local copies, waits for them, and re-layouts  1.69 us
    pallas_call x1, Pallas kernels, merge_inner(): pl.pallas_call(body, out_shape=(array(2, CH, LANES), array(2, 2 * CH, LAN...  1.47 us
    ppermute x3, waiting for transfers between devices, swapped(): lax.ppermute(block, 'frame', [(i, i ^ mask * quarter) for i in range(coun...  1.09 us
  transfers between devices with their start and end apart: 7, of which 3 were waited for; matrix products, arithmetic and copies ran while one was open for 0% of the time, Pallas kernels for 6%

profile of v2, /device:TPU:57, one launch (start us, length us, event | category | flops | bytes accessed | tf_op | source)
XLA Modules:
  0.0 41.5 jit_solution(6048398454221097667)
XLA Ops:
  0.0 0.0 copy-start
  0.0 1.0 %copy-done = bf16[4,64,8,128]{3,2,1,0:T(8,128)(2,1)S(1)} copy-done((bf16[4,64,8,128]{3,2,1,0:T(8,128)(2,1)S(1)}, bf16[4,64,8,128]{3,2,1,0:T(8,128)(2,1)}, u32[]{:S(2)}) %copy-start) | copy-done | bytes 524312
  1.0 0.2 spread.1
  1.3 10.6 %collective-permute-start.3 = (bf16[8,64,128]{2,1,0:T(8,128)(2,1)S(1)}, bf16[8,64,128]{2,1,0:T(8,128)(2,1)S(1)}, u32[]{:S(2)}, u32[]{:S(2)}) collective-permute-start(bf16[8,64,128]{2,1,0:T(8,128)(2,1)S(1)} %get-tuple-element.24), channel_id=1, source_target_pairs={{0,8},{1,9},{2,10},{3,11},{4,12},{5,13},{6,14},{7,15},{8,0},{9,1},... | collective-permute-start | bytes 393224 | tf_op jit(solution)/shard_map/ppermute | solution.py:260
  11.9 4.0 %collective-permute-start = (bf16[8,64,128]{2,1,0:T(8,128)(2,1)S(1)}, bf16[8,64,128]{2,1,0:T(8,128)(2,1)S(1)}, u32[]{:S(2)}, u32[]{:S(2)}) collective-permute-start(bf16[8,64,128]{2,1,0:T(8,128)(2,1)S(1)} %get-tuple-element.20), channel_id=1, source_target_pairs={{0,4},{1,5},{2,6},{3,7},{4,0},{5,1},{6,2},{7,3},{8,12},{9,13},{10,... | collective-permute-start | bytes 393224 | tf_op jit(solution)/shard_map/ppermute | solution.py:260
  15.9 1.9 %collective-permute-start.1 = (bf16[8,64,128]{2,1,0:T(8,128)(2,1)S(1)}, bf16[8,64,128]{2,1,0:T(8,128)(2,1)S(1)}, u32[]{:S(2)}, u32[]{:S(2)}) collective-permute-start(bf16[8,64,128]{2,1,0:T(8,128)(2,1)S(1)} %get-tuple-element.21), channel_id=1, source_target_pairs={{0,12},{1,13},{2,14},{3,15},{4,8},{5,9},{6,10},{7,11},{8,4},{9,5},... | collective-permute-start | bytes 393224 | tf_op jit(solution)/shard_map/ppermute | solution.py:260
  17.9 0.0 collective-permute-done.3.refs_1_.two_r
  17.9 0.0 copy-start.2
  17.9 0.0 copy-start.1
  17.9 3.3 %collective-permute-start.4 = (bf16[4,128,128]{2,1,0:T(8,128)(2,1)S(1)}, bf16[4,128,128]{2,1,0:T(8,128)(2,1)S(1)}, u32[]{:S(2)}, u32[]{:S(2)}) collective-permute-start(bf16[4,128,128]{2,1,0:T(8,128)(2,1)S(1)} %get-tuple-element.25), channel_id=1, source_target_pairs={{0,16},{16,0},{32,48},{48,32},{64,80},{80,64},{96,112},{112,96},{1... | collective-permute-start | bytes 393224 | tf_op jit(solution)/shard_map/ppermute | solution.py:263
  21.2 3.8 %collective-permute-start.5 = (bf16[4,128,128]{2,1,0:T(8,128)(2,1)S(1)}, bf16[4,128,128]{2,1,0:T(8,128)(2,1)S(1)}, u32[]{:S(2)}, u32[]{:S(2)}) collective-permute-start(bf16[4,128,128]{2,1,0:T(8,128)(2,1)S(1)} %get-tuple-element.26), channel_id=1, source_target_pairs={{16,32},{32,16},{48,64},{64,48},{80,96},{96,80},{112,128},{128,112... | collective-permute-start | bytes 393224 | tf_op jit(solution)/shard_map/ppermute | solution.py:266
  25.0 0.5 %collective-permute-done.refs_0_.one_r = bf16[8,64,128]{2,1,0:T(8,128)(2,1)S(1)} collective-permute-done((bf16[8,64,128]{2,1,0:T(8,128)(2,1)S(1)}, bf16[8,64,128]{2,1,0:T(8,128)(2,1)S(1)}, u32[]{:S(2)}, u32[]{:S(2)}) %collective-permute-start) | collective-permute-done | bytes 131104 | tf_op jit(solution)/shard_map/ppermute | solution.py:260
  25.5 0.6 %collective-permute-done.1.refs_1_.three_r = bf16[8,64,128]{2,1,0:T(8,128)(2,1)S(1)} collective-permute-done((bf16[8,64,128]{2,1,0:T(8,128)(2,1)S(1)}, bf16[8,64,128]{2,1,0:T(8,128)(2,1)S(1)}, u32[]{:S(2)}, u32[]{:S(2)}) %collective-permute-start.1) | collective-permute-done | bytes 131104 | tf_op jit(solution)/shard_map/ppermute | solution.py:260
  26.1 3.6 %collective-permute-start.6 = (bf16[4,128,128]{2,1,0:T(8,128)(2,1)S(1)}, bf16[4,128,128]{2,1,0:T(8,128)(2,1)S(1)}, u32[]{:S(2)}, u32[]{:S(2)}) collective-permute-start(bf16[4,128,128]{2,1,0:T(8,128)(2,1)S(1)} %get-tuple-element.30), channel_id=1, source_target_pairs={{0,16},{16,0},{32,48},{48,32},{64,80},{80,64},{96,112},{112,96},{1... | collective-permute-start | bytes 393224 | tf_op jit(solution)/shard_map/ppermute | solution.py:263
  29.7 3.8 %collective-permute-start.2 = (bf16[4,128,128]{2,1,0:T(8,128)(2,1)S(1)}, bf16[4,128,128]{2,1,0:T(8,128)(2,1)S(1)}, u32[]{:S(2)}, u32[]{:S(2)}) collective-permute-start(bf16[4,128,128]{2,1,0:T(8,128)(2,1)S(1)} %get-tuple-element.22), channel_id=1, source_target_pairs={{16,32},{32,16},{48,64},{64,48},{80,96},{96,80},{112,128},{128,112... | collective-permute-start | bytes 393224 | tf_op jit(solution)/shard_map/ppermute | solution.py:266
  33.5 0.0 copy-start.3
  33.5 0.0 copy-start.4
  33.5 0.0 copy-done.2
  33.5 0.0 copy-done.1
  33.5 0.6 %copy-done.3 = f32[64]{0:T(128)S(1)} copy-done((f32[64]{0:T(128)S(1)}, f32[64]{0:T(128)}, u32[]{:S(2)}) %copy-start.3) | copy-done | bytes 280
  34.1 0.0 copy-done.4
  34.1 0.2 weights.1
  34.3 0.0 collective-permute-done.4.near_r
  34.3 0.0 collective-permute-done.5.far_r
  34.3 1.0 %merge_own.1.mine_r = bf16[12,64,128]{2,1,0:T(8,128)(2,1)S(1)} custom-call(bf16[4,128,128]{2,1,0:T(8,128)(2,1)S(1)} %collective-permute-done.4.near_r, bf16[4,128,128]{2,1,0:T(8,128)(2,1)S(1)} %collective-permute-done.5.far_r, bf16[8,64,128]{2,1,0:T(8,128)(2,1)S(1)} %get-tuple-element.23.refs_0_.own_r, ...), custom_call_target="tpu_custom_call" | custom-call | tf_op jit(solution)/shard_map/merge_own/pallas_call | solution.py:164
  35.3 0.0 collective-permute-done.6.near_r
  35.3 1.5 %merge_inner.1 = (bf16[2,64,128]{2,1,0:T(8,128)(2,1)S(1)}, bf16[2,128,128]{2,1,0:T(8,128)(2,1)S(1)}, bf16[2,64,128]{2,1,0:T(8,128)(2,1)S(1)}, f32[4,64,128]{2,1,0:T(8,128)S(1)}) custom-call(bf16[4,128,128]{2,1,0:T(8,128)(2,1)S(1)} %collective-permute-done.6.near_r, bf16[8,64,128]{2,1,0:T(8,128)(2,1)S(1)} %collective-permute-done.refs_0_.one_r, ...), custom_call_target="tpu_custom_call" | custom-call | tf_op jit(solution)/shard_map/merge_inner/pallas_call | solution.py:192
  36.8 2.8 %collective-permute-done.2.far_r = bf16[4,128,128]{2,1,0:T(8,128)(2,1)S(1)} collective-permute-done((bf16[4,128,128]{2,1,0:T(8,128)(2,1)S(1)}, bf16[4,128,128]{2,1,0:T(8,128)(2,1)S(1)}, u32[]{:S(2)}, u32[]{:S(2)}) %collective-permute-start.2) | collective-permute-done | bytes 131104 | tf_op jit(solution)/shard_map/ppermute | solution.py:266
  39.6 1.9 %merge_outer.1 = bf16[64,8,128]{2,1,0:T(8,128)(2,1)} custom-call(bf16[4,128,128]{2,1,0:T(8,128)(2,1)S(1)} %collective-permute-done.2.far_r, bf16[8,64,128]{2,1,0:T(8,128)(2,1)S(1)} %collective-permute-done.refs_0_.one_r, bf16[8,64,128]{2,1,0:T(8,128)(2,1)S(1)} %collective-permute-done.1.refs_1_.three_r, bf16[12,64,128]{2,1,0:T(8,128)(2,1)S(1)} %merge_own.1.mine_r, ...), custom_call_target="tpu_custom_call" | custom-call | tf_op jit(solution)/shard_map/merge_outer/pallas_call | solution.py:234
  (2 shorter events, 0.0 us)
Async XLA Ops:
  0.0 1.0 %copy-start = (bf16[4,64,8,128]{3,2,1,0:T(8,128)(2,1)S(1)}, bf16[4,64,8,128]{3,2,1,0:T(8,128)(2,1)}, u32[]{:S(2)}) copy-start(bf16[4,64,8,128]{3,2,1,0:T(8,128)(2,1)} %src.1) | copy-start | bytes 1572868
  1.3 16.6 %collective-permute-start.3 = (bf16[8,64,128]{2,1,0:T(8,128)(2,1)S(1)}, bf16[8,64,128]{2,1,0:T(8,128)(2,1)S(1)}, u32[]{:S(2)}, u32[]{:S(2)}) collective-permute-start(bf16[8,64,128]{2,1,0:T(8,128)(2,1)S(1)} %get-tuple-element.24), channel_id=1, source_target_pairs={{0,8},{1,9},{2,10},{3,11},{4,12},{5,13},{6,14},{7,15},{8,0},{9,1},... | collective-permute-start | bytes 393224 | tf_op jit(solution)/shard_map/ppermute | solution.py:260
  11.9 13.5 %collective-permute-start = (bf16[8,64,128]{2,1,0:T(8,128)(2,1)S(1)}, bf16[8,64,128]{2,1,0:T(8,128)(2,1)S(1)}, u32[]{:S(2)}, u32[]{:S(2)}) collective-permute-start(bf16[8,64,128]{2,1,0:T(8,128)(2,1)S(1)} %get-tuple-element.20), channel_id=1, source_target_pairs={{0,4},{1,5},{2,6},{3,7},{4,0},{5,1},{6,2},{7,3},{8,12},{9,13},{10,... | collective-permute-start | bytes 393224 | tf_op jit(solution)/shard_map/ppermute | solution.py:260
  15.9 10.1 %collective-permute-start.1 = (bf16[8,64,128]{2,1,0:T(8,128)(2,1)S(1)}, bf16[8,64,128]{2,1,0:T(8,128)(2,1)S(1)}, u32[]{:S(2)}, u32[]{:S(2)}) collective-permute-start(bf16[8,64,128]{2,1,0:T(8,128)(2,1)S(1)} %get-tuple-element.21), channel_id=1, source_target_pairs={{0,12},{1,13},{2,14},{3,15},{4,8},{5,9},{6,10},{7,11},{8,4},{9,5},... | collective-permute-start | bytes 393224 | tf_op jit(solution)/shard_map/ppermute | solution.py:260
  17.9 15.6 %copy-start.2 = (bf16[3,3,64,64]{3,2,1,0:T(8,128)(2,1)S(1)}, bf16[3,3,64,64]{3,2,1,0:T(8,128)(2,1)}, u32[]{:S(2)}) copy-start(bf16[3,3,64,64]{3,2,1,0:T(8,128)(2,1)} %param.7) | copy-start | bytes 221188
  17.9 15.6 %copy-start.1 = (bf16[3,3,64,128]{3,2,1,0:T(8,128)(2,1)S(1)}, bf16[3,3,64,128]{3,2,1,0:T(8,128)(2,1)}, u32[]{:S(2)}) copy-start(bf16[3,3,64,128]{3,2,1,0:T(8,128)(2,1)} %param.6) | copy-start | bytes 442372
  17.9 16.4 %collective-permute-start.4 = (bf16[4,128,128]{2,1,0:T(8,128)(2,1)S(1)}, bf16[4,128,128]{2,1,0:T(8,128)(2,1)S(1)}, u32[]{:S(2)}, u32[]{:S(2)}) collective-permute-start(bf16[4,128,128]{2,1,0:T(8,128)(2,1)S(1)} %get-tuple-element.25), channel_id=1, source_target_pairs={{0,16},{16,0},{32,48},{48,32},{64,80},{80,64},{96,112},{112,96},{1... | collective-permute-start | bytes 393224 | tf_op jit(solution)/shard_map/ppermute | solution.py:263
  21.2 13.1 %collective-permute-start.5 = (bf16[4,128,128]{2,1,0:T(8,128)(2,1)S(1)}, bf16[4,128,128]{2,1,0:T(8,128)(2,1)S(1)}, u32[]{:S(2)}, u32[]{:S(2)}) collective-permute-start(bf16[4,128,128]{2,1,0:T(8,128)(2,1)S(1)} %get-tuple-element.26), channel_id=1, source_target_pairs={{16,32},{32,16},{48,64},{64,48},{80,96},{96,80},{112,128},{128,112... | collective-permute-start | bytes 393224 | tf_op jit(solution)/shard_map/ppermute | solution.py:266
  26.1 9.2 %collective-permute-start.6 = (bf16[4,128,128]{2,1,0:T(8,128)(2,1)S(1)}, bf16[4,128,128]{2,1,0:T(8,128)(2,1)S(1)}, u32[]{:S(2)}, u32[]{:S(2)}) collective-permute-start(bf16[4,128,128]{2,1,0:T(8,128)(2,1)S(1)} %get-tuple-element.30), channel_id=1, source_target_pairs={{0,16},{16,0},{32,48},{48,32},{64,80},{80,64},{96,112},{112,96},{1... | collective-permute-start | bytes 393224 | tf_op jit(solution)/shard_map/ppermute | solution.py:263
  29.7 9.9 %collective-permute-start.2 = (bf16[4,128,128]{2,1,0:T(8,128)(2,1)S(1)}, bf16[4,128,128]{2,1,0:T(8,128)(2,1)S(1)}, u32[]{:S(2)}, u32[]{:S(2)}) collective-permute-start(bf16[4,128,128]{2,1,0:T(8,128)(2,1)S(1)} %get-tuple-element.22), channel_id=1, source_target_pairs={{16,32},{32,16},{48,64},{64,48},{80,96},{96,80},{112,128},{128,112... | collective-permute-start | bytes 393224 | tf_op jit(solution)/shard_map/ppermute | solution.py:266
  33.5 0.7 %copy-start.3 = (f32[64]{0:T(128)S(1)}, f32[64]{0:T(128)}, u32[]{:S(2)}) copy-start(f32[64]{0:T(128)} %param.8) | copy-start | bytes 772
  33.5 0.7 %copy-start.4 = (f32[64]{0:T(128)S(1)}, f32[64]{0:T(128)}, u32[]{:S(2)}) copy-start(f32[64]{0:T(128)} %param.9) | copy-start | bytes 772

commit v3 on v1

--- a/solution.py
+++ b/solution.py
@@ -1,3 +1,5 @@
+from functools import partial
+
 import jax
 import jax.numpy as jnp
 from jax import lax
@@ -10,6 +12,7 @@
 HALO = 4
 CH = 64
 LANES = 128
+FRONT = 54800
 VMEM = pl.BlockSpec(memory_space=pltpu.VMEM)
 SMALL = pltpu.CompilerParams(vmem_limit_bytes=8 << 20)
 
@@ -26,21 +29,47 @@
     return lax.axis_index("row") % 2
 
 
+def lead(frames):
+    def body(src, two, held, wide, sem):
+        copy = pltpu.make_async_copy(src.at[position() ^ 2], held, sem)
+        copy.start()
+        copy.wait()
+        rows_first(held[...], wide, two)
+
+    return pl.pallas_call(
+        body,
+        out_shape=array(ROWS, CH, LANES),
+        in_specs=[pl.BlockSpec(memory_space=pl.ANY)],
+        out_specs=VMEM,
+        scratch_shapes=[
+            pltpu.VMEM((CH, ROWS, LANES), jnp.bfloat16),
+            pltpu.VMEM((CH * ROWS, LANES), jnp.float32),
+            pltpu.SemaphoreType.DMA,
+        ],
+        compiler_params=pltpu.CompilerParams(vmem_limit_bytes=FRONT << 10),
+        name="lead",
+    )(frames)
+
+
+def rows_first(frame, wide, out):
+    wide[...] = frame.astype(jnp.float32).reshape(CH * ROWS, LANES)
+    turn = 7 - 7 * odd_row()
+    sign = 2 * odd_row() - 1
+    for row in range(ROWS):
+        out[turn + sign * row] = wide[pl.ds(row, CH, stride=ROWS), :].astype(jnp.bfloat16)
+
+
 def spread(frames):
-    def body(src, own, one, three, two, wide):
+    def body(src, own, one, three, wide):
         at = position()
-        turn = 7 - 7 * odd_row()
-        sign = 2 * odd_row() - 1
-        for k, out in ((2, two), (1, one), (3, three), (0, own)):
-            wide[k] = src[at ^ k].astype(jnp.float32).reshape(CH * ROWS, LANES)
-            for row in range(ROWS):
-                out[turn + sign * row] = wide[k, pl.ds(row, CH, stride=ROWS), :].astype(jnp.bfloat16)
-
-    return pl.pallas_call(
-        body,
-        out_shape=(array(ROWS, CH, LANES),) * 4,
+        for k, out in ((1, one), (3, three), (0, own)):
+            rows_first(src[at ^ k], wide.at[k], out)
+
+    return pl.pallas_call(
+        body,
+        out_shape=(array(ROWS, CH, LANES),) * 3,
         in_specs=[VMEM],
-        out_specs=(VMEM,) * 4,
+        out_specs=(VMEM,) * 3,
         scratch_shapes=[pltpu.VMEM((4, CH * ROWS, LANES), jnp.float32)],
         compiler_params=SMALL,
         name="spread",
@@ -96,6 +125,12 @@
     stack[at : at + source.shape[0], to, :] = source[:, part * CH : (part + 1) * CH, :]
 
 
+def at_seam():
+    row = lax.axis_index("row")
+    half = lax.axis_size("row") // 2
+    return (row == half) | (row == half - 1)
+
+
 class Level:
     def __init__(self, pair, mixed, cols, swap, hid):
         lane = lax.broadcasted_iota(jnp.int32, (CH, LANES), 1)
@@ -172,7 +207,10 @@
 
 
 def merge_inner(near_side, one, three, mine, tables):
-    def body(near_r, one_r, three_r, mine_r, pair, mixed, cols, hid_end, ones_end, top_end, done, stack, ones, hid, top_hid):
+    def body(*refs):
+        pl.when(at_seam())(partial(inner, *refs))
+
+    def inner(near_r, one_r, three_r, mine_r, pair, mixed, cols, hid_end, ones_end, top_end, done, stack, ones, hid, top_hid):
         for slot, frame in enumerate((one_r, three_r)):
             fill(stack, slot, near_r, 0, slot)
             fill(stack, slot, frame, HALO)
@@ -199,23 +237,41 @@
     )(near_side, one, three, mine, *tables)
 
 
-def merge_outer(far_side, one, three, mine, inner, tables):
-    def body(far_r, one_r, three_r, mine_r, hid_end, ones_end, top_end, done, pair, mixed, cols, out, stack, ones, hid, top_hid, rows, wide):
-        for slot, frame in enumerate((one_r, three_r)):
-            fill(stack, slot, frame.at[6:8], 10)
-            fill(stack, slot, far_r, HALO + ROWS, slot)
-        hid[9:11] = hid_end[...]
-        ones[8:10] = ones_end[...]
-        fill(ones, 0, mine_r.at[8:12], 10)
-        top_hid[7:9] = top_end[...]
-        rows[0:4] = done[...]
+def merge_outer(near_side, far_side, one, three, mine, inner, tables):
+    def body(near_r, far_r, one_r, three_r, mine_r, hid_end, ones_end, top_end, done, pair, mixed, cols, out, stack, ones, hid, top_hid, rows, wide):
         at = position()
-        level = Level(pair, mixed, cols, at // 2, hid)
-        level.first(stack, 0, 11, 15)
-        level.second(stack, 0, 10, 14, into(ones, 0, OTHER))
-        top = Level(pair, mixed, cols, at % 2, top_hid)
-        top.first(ones, 0, 9, 13)
-        top.second(ones, 0, 8, 12, into(rows, 4, slice(None)))
+
+        @pl.when(at_seam())
+        def _():
+            for slot, frame in enumerate((one_r, three_r)):
+                fill(stack, slot, frame.at[6:8], 10)
+                fill(stack, slot, far_r, HALO + ROWS, slot)
+            hid[9:11] = hid_end[...]
+            ones[8:10] = ones_end[...]
+            fill(ones, 0, mine_r.at[8:12], 10)
+            top_hid[7:9] = top_end[...]
+            rows[0:4] = done[...]
+            level = Level(pair, mixed, cols, at // 2, hid)
+            level.first(stack, 0, 11, 15)
+            level.second(stack, 0, 10, 14, into(ones, 0, OTHER))
+            top = Level(pair, mixed, cols, at % 2, top_hid)
+            top.first(ones, 0, 9, 13)
+            top.second(ones, 0, 8, 12, into(rows, 4, slice(None)))
+
+        @pl.when(jnp.logical_not(at_seam()))
+        def _():
+            for slot, frame in enumerate((one_r, three_r)):
+                fill(stack, slot, near_r, 0, slot)
+                fill(stack, slot, frame, HALO)
+                fill(stack, slot, far_r, HALO + ROWS, slot)
+            fill(ones, 0, mine_r, 2)
+            level = Level(pair, mixed, cols, at // 2, hid)
+            level.first(stack, 0, 1, 15)
+            level.second(stack, 0, 2, 14, into(ones, 0, OTHER))
+            top = Level(pair, mixed, cols, at % 2, top_hid)
+            top.first(ones, 0, 3, 13)
+            top.second(ones, 0, 4, 12, into(rows, 4, slice(None)))
+
         turn = 7 - 7 * odd_row()
         sign = 2 * odd_row() - 1
         for row in range(ROWS):
@@ -225,7 +281,7 @@
     return pl.pallas_call(
         body,
         out_shape=array(CH, ROWS, LANES),
-        in_specs=[VMEM] * 11,
+        in_specs=[VMEM] * 12,
         scratch_shapes=[
             STACK,
             STACK,
@@ -236,7 +292,7 @@
         ],
         compiler_params=SMALL,
         name="merge_outer",
-    )(far_side, one, three, mine, *inner, *tables)
+    )(near_side, far_side, one, three, mine, *inner, *tables)
 
 
 def on_device(frames, w_pair, w_mixed, slope_pair, slope_mixed):
@@ -253,7 +309,8 @@
     def off_chip(block):
         return lax.ppermute(block, "row", [(i, ((i + 1) ^ 1) - 1) for i in range(1, rows - 1)])
 
-    own, one, three, two = spread(frames)
+    two = lead(frames)
+    own, one, three = spread(frames)
     one = swapped(one, 1)
     three = swapped(three, 3)
     two = swapped(two, 2)
@@ -266,7 +323,7 @@
     near_late = on_chip(near_late)
     mine = merge_own(near_early, far_early, own, two, tables)
     inner = merge_inner(near_late, one, three, mine, tables)
-    merged = merge_outer(far_late, one, three, mine, inner, tables)
+    merged = merge_outer(near_late, far_late, one, three, mine, inner, tables)
     return merged[None]
 
 

time: 41.9 us -> 42 us (level)
  local copies, waits for them, and re-layouts: 1.69 us -> 0.65 us
  Pallas kernels: 4.84 us -> 5.87 us
    unnamed x10, local copies, waits for them, and re-layouts: 1.69 us -> 0.65 us
    pallas_call x1 -> x2, Pallas kernels: 0.24 us -> 1.24 us  [the longest x1 1.05 us: lead(): pl.pallas_call(body, out_shape=array(ROWS, CH, LANES), in_specs=[pl.Block...]
  transfers between devices with their start and end apart: 7 -> 7, of which waited for: 3 -> 3; matrix products, arithmetic and copies ran while one was open for 0% -> 0% of each run, Pallas kernels for 6% -> 7%
where the time goes in v3:
time: 42 us; the launch traced here: 41.8 us
  starting transfers between devices  30.7 us (73%)
  Pallas kernels  5.87 us (14%)
  waiting for transfers between devices  4.3 us (10%)
  local copies, waits for them, and re-layouts  0.65 us (2%)
    ppermute x3, starting transfers between devices, swapped(): lax.ppermute(block, 'frame', [(i, i ^ mask * quarter) for i in range(coun...  16.6 us
    ppermute x2, starting transfers between devices, off_chip(): lax.ppermute(block, 'row', [(i, (i + 1 ^ 1) - 1) for i in range(1, rows -...  7.51 us
    ppermute x2, starting transfers between devices, on_chip(): return lax.ppermute(block, 'row', [(i, i ^ 1) for i in range(rows)])  6.66 us
    ppermute x2, waiting for transfers between devices, off_chip(): lax.ppermute(block, 'row', [(i, (i + 1 ^ 1) - 1) for i in range(1, rows -...  2.79 us
    pallas_call x1, Pallas kernels, merge_outer(): pl.pallas_call(body, out_shape=array(CH, ROWS, LANES), in_specs=[VMEM] *...  1.97 us
    ppermute x3, waiting for transfers between devices, swapped(): lax.ppermute(block, 'frame', [(i, i ^ mask * quarter) for i in range(coun...  1.5 us
    pallas_call x1, Pallas kernels, merge_inner(): pl.pallas_call(body, out_shape=(array(2, CH, LANES), array(2, 2 * CH, LAN...  1.48 us
    pallas_call x1, Pallas kernels, lead(): pl.pallas_call(body, out_shape=array(ROWS, CH, LANES), in_specs=[pl.Block...  1.05 us
  transfers between devices with their start and end apart: 7, of which 3 were waited for; matrix products, arithmetic and copies ran while one was open for 0% of the time, Pallas kernels for 7%

profile of v3, /device:TPU:57, one launch (start us, length us, event | category | flops | bytes accessed | tf_op | source)
XLA Modules:
  0.0 41.8 jit_solution(3342045362425362720)
XLA Ops:
  0.0 0.0 copy-start
  0.0 1.0 %lead.1 = bf16[8,64,128]{2,1,0:T(8,128)(2,1)S(1)} custom-call(bf16[4,64,8,128]{3,2,1,0:T(8,128)(2,1)} %src.3), custom_call_target="tpu_custom_call" | custom-call | tf_op jit(solution)/shard_map/lead/pallas_call | solution.py:39
  1.1 10.6 %collective-permute-start.4 = (bf16[8,64,128]{2,1,0:T(8,128)(2,1)S(1)}, bf16[8,64,128]{2,1,0:T(8,128)(2,1)S(1)}, u32[]{:S(2)}, u32[]{:S(2)}) collective-permute-start(bf16[8,64,128]{2,1,0:T(8,128)(2,1)S(1)} %lead.1), channel_id=1, source_target_pairs={{0,8},{1,9},{2,10},{3,11},{4,12},{5,13},{6,14},{7,15},{8,0},{9,1},... | collective-permute-start | bytes 393224 | tf_op jit(solution)/shard_map/ppermute | solution.py:304
  11.7 0.0 copy-done
  11.7 0.2 spread.1
  11.9 4.0 %collective-permute-start = (bf16[8,64,128]{2,1,0:T(8,128)(2,1)S(1)}, bf16[8,64,128]{2,1,0:T(8,128)(2,1)S(1)}, u32[]{:S(2)}, u32[]{:S(2)}) collective-permute-start(bf16[8,64,128]{2,1,0:T(8,128)(2,1)S(1)} %get-tuple-element.19), channel_id=1, source_target_pairs={{0,4},{1,5},{2,6},{3,7},{4,0},{5,1},{6,2},{7,3},{8,12},{9,13},{10,... | collective-permute-start | bytes 393224 | tf_op jit(solution)/shard_map/ppermute | solution.py:304
  15.9 1.9 %collective-permute-start.1 = (bf16[8,64,128]{2,1,0:T(8,128)(2,1)S(1)}, bf16[8,64,128]{2,1,0:T(8,128)(2,1)S(1)}, u32[]{:S(2)}, u32[]{:S(2)}) collective-permute-start(bf16[8,64,128]{2,1,0:T(8,128)(2,1)S(1)} %get-tuple-element.20), channel_id=1, source_target_pairs={{0,12},{1,13},{2,14},{3,15},{4,8},{5,9},{6,10},{7,11},{8,4},{9,5},... | collective-permute-start | bytes 393224 | tf_op jit(solution)/shard_map/ppermute | solution.py:304
  17.9 0.0 collective-permute-done.4.refs_1_.two_r
  17.9 0.0 copy-start.2
  17.9 0.0 copy-start.1
  17.9 3.3 %collective-permute-start.5 = (bf16[4,128,128]{2,1,0:T(8,128)(2,1)S(1)}, bf16[4,128,128]{2,1,0:T(8,128)(2,1)S(1)}, u32[]{:S(2)}, u32[]{:S(2)}) collective-permute-start(bf16[4,128,128]{2,1,0:T(8,128)(2,1)S(1)} %get-tuple-element.24), channel_id=1, source_target_pairs={{0,16},{16,0},{32,48},{48,32},{64,80},{80,64},{96,112},{112,96},{1... | collective-permute-start | bytes 393224 | tf_op jit(solution)/shard_map/ppermute | solution.py:307
  21.2 3.8 %collective-permute-start.6 = (bf16[4,128,128]{2,1,0:T(8,128)(2,1)S(1)}, bf16[4,128,128]{2,1,0:T(8,128)(2,1)S(1)}, u32[]{:S(2)}, u32[]{:S(2)}) collective-permute-start(bf16[4,128,128]{2,1,0:T(8,128)(2,1)S(1)} %get-tuple-element.25), channel_id=1, source_target_pairs={{16,32},{32,16},{48,64},{64,48},{80,96},{96,80},{112,128},{128,112... | collective-permute-start | bytes 393224 | tf_op jit(solution)/shard_map/ppermute | solution.py:310
  25.0 0.3 collective-permute-done.refs_0_.refs_1_.one_r
  25.2 1.2 %collective-permute-done.1.refs_1_.refs_2_.three_r = bf16[8,64,128]{2,1,0:T(8,128)(2,1)S(1)} collective-permute-done((bf16[8,64,128]{2,1,0:T(8,128)(2,1)S(1)}, bf16[8,64,128]{2,1,0:T(8,128)(2,1)S(1)}, u32[]{:S(2)}, u32[]{:S(2)}) %collective-permute-start.1) | collective-permute-done | bytes 131104 | tf_op jit(solution)/shard_map/ppermute | solution.py:304
  26.5 3.4 %collective-permute-start.2 = (bf16[4,128,128]{2,1,0:T(8,128)(2,1)S(1)}, bf16[4,128,128]{2,1,0:T(8,128)(2,1)S(1)}, u32[]{:S(2)}, u32[]{:S(2)}) collective-permute-start(bf16[4,128,128]{2,1,0:T(8,128)(2,1)S(1)} %get-tuple-element.21), channel_id=1, source_target_pairs={{0,16},{16,0},{32,48},{48,32},{64,80},{80,64},{96,112},{112,96},{1... | collective-permute-start | bytes 393224 | tf_op jit(solution)/shard_map/ppermute | solution.py:307
  29.9 3.8 %collective-permute-start.3 = (bf16[4,128,128]{2,1,0:T(8,128)(2,1)S(1)}, bf16[4,128,128]{2,1,0:T(8,128)(2,1)S(1)}, u32[]{:S(2)}, u32[]{:S(2)}) collective-permute-start(bf16[4,128,128]{2,1,0:T(8,128)(2,1)S(1)} %get-tuple-element.22), channel_id=1, source_target_pairs={{16,32},{32,16},{48,64},{64,48},{80,96},{96,80},{112,128},{128,112... | collective-permute-start | bytes 393224 | tf_op jit(solution)/shard_map/ppermute | solution.py:310
  33.6 0.0 copy-start.3
  33.7 0.0 copy-start.4
  33.7 0.0 copy-done.2
  33.7 0.0 copy-done.1
  33.7 0.6 %copy-done.3 = f32[64]{0:T(128)S(1)} copy-done((f32[64]{0:T(128)S(1)}, f32[64]{0:T(128)}, u32[]{:S(2)}) %copy-start.3) | copy-done | bytes 280
  34.3 0.0 copy-done.4
  34.3 0.2 weights.1
  34.5 0.0 collective-permute-done.5.near_r
  34.5 0.0 collective-permute-done.6.far_r
  34.5 1.0 %merge_own.1.refs_3_.mine_r = bf16[12,64,128]{2,1,0:T(8,128)(2,1)S(1)} custom-call(bf16[4,128,128]{2,1,0:T(8,128)(2,1)S(1)} %collective-permute-done.5.near_r, bf16[4,128,128]{2,1,0:T(8,128)(2,1)S(1)} %collective-permute-done.6.far_r, bf16[8,64,128]{2,1,0:T(8,128)(2,1)S(1)} %get-tuple-element.23.refs_0_.own_r, ...), custom_call_target="tpu_custom_call" | custom-call | tf_op jit(solution)/shard_map/merge_own/pallas_call | solution.py:198
  35.5 0.0 collective-permute-done.2.refs_0_.near_r
  35.5 1.5 %merge_inner.1 = (bf16[2,64,128]{2,1,0:T(8,128)(2,1)S(1)}, bf16[2,128,128]{2,1,0:T(8,128)(2,1)S(1)}, bf16[2,64,128]{2,1,0:T(8,128)(2,1)S(1)}, f32[4,64,128]{2,1,0:T(8,128)S(1)}) custom-call(bf16[4,128,128]{2,1,0:T(8,128)(2,1)S(1)} %collective-permute-done.2.refs_0_.near_r, bf16[8,64,128]{2,1,0:T(8,128)(2,1)S(1)} %collective-permute-done.refs_0_.refs_1_.one_r, ...), custom_call_target="tpu_custom_call" | custom-call | tf_op jit(solution)/shard_map/merge_inner/pallas_call | solution.py:229
  37.0 2.8 %collective-permute-done.3.far_r = bf16[4,128,128]{2,1,0:T(8,128)(2,1)S(1)} collective-permute-done((bf16[4,128,128]{2,1,0:T(8,128)(2,1)S(1)}, bf16[4,128,128]{2,1,0:T(8,128)(2,1)S(1)}, u32[]{:S(2)}, u32[]{:S(2)}) %collective-permute-start.3) | collective-permute-done | bytes 131104 | tf_op jit(solution)/shard_map/ppermute | solution.py:310
  39.8 2.0 %merge_outer.1 = bf16[64,8,128]{2,1,0:T(8,128)(2,1)} custom-call(bf16[4,128,128]{2,1,0:T(8,128)(2,1)S(1)} %collective-permute-done.2.refs_0_.near_r, bf16[4,128,128]{2,1,0:T(8,128)(2,1)S(1)} %collective-permute-done.3.far_r, bf16[8,64,128]{2,1,0:T(8,128)(2,1)S(1)} %collective-permute-done.refs_0_.refs_1_.one_r, ...), custom_call_target="tpu_custom_call" | custom-call | tf_op jit(solution)/shard_map/merge_outer/pallas_call | solution.py:281
  (2 shorter events, 0.0 us)
Async XLA Ops:
  0.0 11.7 %copy-start = (bf16[4,64,8,128]{3,2,1,0:T(8,128)(2,1)S(1)}, bf16[4,64,8,128]{3,2,1,0:T(8,128)(2,1)}, u32[]{:S(2)}) copy-start(bf16[4,64,8,128]{3,2,1,0:T(8,128)(2,1)} %src.3) | copy-start | bytes 1572868
  1.1 16.8 %collective-permute-start.4 = (bf16[8,64,128]{2,1,0:T(8,128)(2,1)S(1)}, bf16[8,64,128]{2,1,0:T(8,128)(2,1)S(1)}, u32[]{:S(2)}, u32[]{:S(2)}) collective-permute-start(bf16[8,64,128]{2,1,0:T(8,128)(2,1)S(1)} %lead.1), channel_id=1, source_target_pairs={{0,8},{1,9},{2,10},{3,11},{4,12},{5,13},{6,14},{7,15},{8,0},{9,1},... | collective-permute-start | bytes 393224 | tf_op jit(solution)/shard_map/ppermute | solution.py:304
  11.9 13.3 %collective-permute-start = (bf16[8,64,128]{2,1,0:T(8,128)(2,1)S(1)}, bf16[8,64,128]{2,1,0:T(8,128)(2,1)S(1)}, u32[]{:S(2)}, u32[]{:S(2)}) collective-permute-start(bf16[8,64,128]{2,1,0:T(8,128)(2,1)S(1)} %get-tuple-element.19), channel_id=1, source_target_pairs={{0,4},{1,5},{2,6},{3,7},{4,0},{5,1},{6,2},{7,3},{8,12},{9,13},{10,... | collective-permute-start | bytes 393224 | tf_op jit(solution)/shard_map/ppermute | solution.py:304
  15.9 10.5 %collective-permute-start.1 = (bf16[8,64,128]{2,1,0:T(8,128)(2,1)S(1)}, bf16[8,64,128]{2,1,0:T(8,128)(2,1)S(1)}, u32[]{:S(2)}, u32[]{:S(2)}) collective-permute-start(bf16[8,64,128]{2,1,0:T(8,128)(2,1)S(1)} %get-tuple-element.20), channel_id=1, source_target_pairs={{0,12},{1,13},{2,14},{3,15},{4,8},{5,9},{6,10},{7,11},{8,4},{9,5},... | collective-permute-start | bytes 393224 | tf_op jit(solution)/shard_map/ppermute | solution.py:304
  17.9 15.8 %copy-start.2 = (bf16[3,3,64,64]{3,2,1,0:T(8,128)(2,1)S(1)}, bf16[3,3,64,64]{3,2,1,0:T(8,128)(2,1)}, u32[]{:S(2)}) copy-start(bf16[3,3,64,64]{3,2,1,0:T(8,128)(2,1)} %param.7) | copy-start | bytes 221188
  17.9 15.8 %copy-start.1 = (bf16[3,3,64,128]{3,2,1,0:T(8,128)(2,1)S(1)}, bf16[3,3,64,128]{3,2,1,0:T(8,128)(2,1)}, u32[]{:S(2)}) copy-start(bf16[3,3,64,128]{3,2,1,0:T(8,128)(2,1)} %param.6) | copy-start | bytes 442372
  17.9 16.6 %collective-permute-start.5 = (bf16[4,128,128]{2,1,0:T(8,128)(2,1)S(1)}, bf16[4,128,128]{2,1,0:T(8,128)(2,1)S(1)}, u32[]{:S(2)}, u32[]{:S(2)}) collective-permute-start(bf16[4,128,128]{2,1,0:T(8,128)(2,1)S(1)} %get-tuple-element.24), channel_id=1, source_target_pairs={{0,16},{16,0},{32,48},{48,32},{64,80},{80,64},{96,112},{112,96},{1... | collective-permute-start | bytes 393224 | tf_op jit(solution)/shard_map/ppermute | solution.py:307
  21.2 13.3 %collective-permute-start.6 = (bf16[4,128,128]{2,1,0:T(8,128)(2,1)S(1)}, bf16[4,128,128]{2,1,0:T(8,128)(2,1)S(1)}, u32[]{:S(2)}, u32[]{:S(2)}) collective-permute-start(bf16[4,128,128]{2,1,0:T(8,128)(2,1)S(1)} %get-tuple-element.25), channel_id=1, source_target_pairs={{16,32},{32,16},{48,64},{64,48},{80,96},{96,80},{112,128},{128,112... | collective-permute-start | bytes 393224 | tf_op jit(solution)/shard_map/ppermute | solution.py:310
  26.5 9.0 %collective-permute-start.2 = (bf16[4,128,128]{2,1,0:T(8,128)(2,1)S(1)}, bf16[4,128,128]{2,1,0:T(8,128)(2,1)S(1)}, u32[]{:S(2)}, u32[]{:S(2)}) collective-permute-start(bf16[4,128,128]{2,1,0:T(8,128)(2,1)S(1)} %get-tuple-element.21), channel_id=1, source_target_pairs={{0,16},{16,0},{32,48},{48,32},{64,80},{80,64},{96,112},{112,96},{1... | collective-permute-start | bytes 393224 | tf_op jit(solution)/shard_map/ppermute | solution.py:307
  29.9 9.9 %collective-permute-start.3 = (bf16[4,128,128]{2,1,0:T(8,128)(2,1)S(1)}, bf16[4,128,128]{2,1,0:T(8,128)(2,1)S(1)}, u32[]{:S(2)}, u32[]{:S(2)}) collective-permute-start(bf16[4,128,128]{2,1,0:T(8,128)(2,1)S(1)} %get-tuple-element.22), channel_id=1, source_target_pairs={{16,32},{32,16},{48,64},{64,48},{80,96},{96,80},{112,128},{128,112... | collective-permute-start | bytes 393224 | tf_op jit(solution)/shard_map/ppermute | solution.py:310
  33.6 0.7 %copy-start.3 = (f32[64]{0:T(128)S(1)}, f32[64]{0:T(128)}, u32[]{:S(2)}) copy-start(f32[64]{0:T(128)} %param.8) | copy-start | bytes 772
  33.7 0.7 %copy-start.4 = (f32[64]{0:T(128)S(1)}, f32[64]{0:T(128)}, u32[]{:S(2)}) copy-start(f32[64]{0:T(128)} %param.9) | copy-start | bytes 772

commit v4 on v3

--- a/solution.py
+++ b/solution.py
@@ -12,6 +12,7 @@
 HALO = 4
 CH = 64
 LANES = 128
+PIECES = 8
 FRONT = 54800
 VMEM = pl.BlockSpec(memory_space=pltpu.VMEM)
 SMALL = pltpu.CompilerParams(vmem_limit_bytes=8 << 20)
@@ -30,10 +31,14 @@
 
 
 def lead(frames):
-    def body(src, two, held, wide, sem):
-        copy = pltpu.make_async_copy(src.at[position() ^ 2], held, sem)
-        copy.start()
-        copy.wait()
+    def body(src, two, held, wide, sems):
+        copies = []
+        for k in range(PIECES):
+            some = pl.ds(k * CH // PIECES, CH // PIECES)
+            copies.append(pltpu.make_async_copy(src.at[position() ^ 2, some], held.at[some], sems.at[k]))
+            copies[k].start()
+        for copy in copies:
+            copy.wait()
         rows_first(held[...], wide, two)
 
     return pl.pallas_call(
@@ -44,7 +49,7 @@
         scratch_shapes=[
             pltpu.VMEM((CH, ROWS, LANES), jnp.bfloat16),
             pltpu.VMEM((CH * ROWS, LANES), jnp.float32),
-            pltpu.SemaphoreType.DMA,
+            pltpu.SemaphoreType.DMA((PIECES,)),
         ],
         compiler_params=pltpu.CompilerParams(vmem_limit_bytes=FRONT << 10),
         name="lead",

time: 42 us -> 42.1 us (level)
  no operation moved by 1% of the time
where the time goes in v4:
time: 42.1 us; the launch traced here: 41.7 us
  starting transfers between devices  30.7 us (73%)
  Pallas kernels  5.85 us (14%)
  waiting for transfers between devices  4.3 us (10%)
  local copies, waits for them, and re-layouts  0.65 us (2%)
    ppermute x3, starting transfers between devices, swapped(): lax.ppermute(block, 'frame', [(i, i ^ mask * quarter) for i in range(coun...  16.6 us
    ppermute x2, starting transfers between devices, off_chip(): lax.ppermute(block, 'row', [(i, (i + 1 ^ 1) - 1) for i in range(1, rows -...  7.51 us
    ppermute x2, starting transfers between devices, on_chip(): return lax.ppermute(block, 'row', [(i, i ^ 1) for i in range(rows)])  6.66 us
    ppermute x2, waiting for transfers between devices, off_chip(): lax.ppermute(block, 'row', [(i, (i + 1 ^ 1) - 1) for i in range(1, rows -...  2.79 us
    pallas_call x1, Pallas kernels, merge_outer(): pl.pallas_call(body, out_shape=array(CH, ROWS, LANES), in_specs=[VMEM] *...  1.97 us
    ppermute x3, waiting for transfers between devices, swapped(): lax.ppermute(block, 'frame', [(i, i ^ mask * quarter) for i in range(coun...  1.5 us
    pallas_call x1, Pallas kernels, merge_inner(): pl.pallas_call(body, out_shape=(array(2, CH, LANES), array(2, 2 * CH, LAN...  1.48 us
    pallas_call x1, Pallas kernels, lead(): pl.pallas_call(body, out_shape=array(ROWS, CH, LANES), in_specs=[pl.Block...  1.02 us
  transfers between devices with their start and end apart: 7, of which 3 were waited for; matrix products, arithmetic and copies ran while one was open for 0% of the time, Pallas kernels for 7%

profile of v4, /device:TPU:57, one launch (start us, length us, event | category | flops | bytes accessed | tf_op | source)
XLA Modules:
  0.0 41.7 jit_solution(15359178475672085197)
XLA Ops:
  0.0 0.0 copy-start
  0.0 1.0 %lead.1 = bf16[8,64,128]{2,1,0:T(8,128)(2,1)S(1)} custom-call(bf16[4,64,8,128]{3,2,1,0:T(8,128)(2,1)} %src.3), custom_call_target="tpu_custom_call" | custom-call | tf_op jit(solution)/shard_map/lead/pallas_call | solution.py:44
  1.0 10.6 %collective-permute-start.4 = (bf16[8,64,128]{2,1,0:T(8,128)(2,1)S(1)}, bf16[8,64,128]{2,1,0:T(8,128)(2,1)S(1)}, u32[]{:S(2)}, u32[]{:S(2)}) collective-permute-start(bf16[8,64,128]{2,1,0:T(8,128)(2,1)S(1)} %lead.1), channel_id=1, source_target_pairs={{0,8},{1,9},{2,10},{3,11},{4,12},{5,13},{6,14},{7,15},{8,0},{9,1},... | collective-permute-start | bytes 393224 | tf_op jit(solution)/shard_map/ppermute | solution.py:309
  11.7 0.0 copy-done
  11.7 0.2 spread.1
  11.9 4.0 %collective-permute-start = (bf16[8,64,128]{2,1,0:T(8,128)(2,1)S(1)}, bf16[8,64,128]{2,1,0:T(8,128)(2,1)S(1)}, u32[]{:S(2)}, u32[]{:S(2)}) collective-permute-start(bf16[8,64,128]{2,1,0:T(8,128)(2,1)S(1)} %get-tuple-element.19), channel_id=1, source_target_pairs={{0,4},{1,5},{2,6},{3,7},{4,0},{5,1},{6,2},{7,3},{8,12},{9,13},{10,... | collective-permute-start | bytes 393224 | tf_op jit(solution)/shard_map/ppermute | solution.py:309
  15.9 1.9 %collective-permute-start.1 = (bf16[8,64,128]{2,1,0:T(8,128)(2,1)S(1)}, bf16[8,64,128]{2,1,0:T(8,128)(2,1)S(1)}, u32[]{:S(2)}, u32[]{:S(2)}) collective-permute-start(bf16[8,64,128]{2,1,0:T(8,128)(2,1)S(1)} %get-tuple-element.20), channel_id=1, source_target_pairs={{0,12},{1,13},{2,14},{3,15},{4,8},{5,9},{6,10},{7,11},{8,4},{9,5},... | collective-permute-start | bytes 393224 | tf_op jit(solution)/shard_map/ppermute | solution.py:309
  17.8 0.0 collective-permute-done.4.refs_1_.two_r
  17.8 0.0 copy-start.2
  17.9 0.0 copy-start.1
  17.9 3.3 %collective-permute-start.5 = (bf16[4,128,128]{2,1,0:T(8,128)(2,1)S(1)}, bf16[4,128,128]{2,1,0:T(8,128)(2,1)S(1)}, u32[]{:S(2)}, u32[]{:S(2)}) collective-permute-start(bf16[4,128,128]{2,1,0:T(8,128)(2,1)S(1)} %get-tuple-element.24), channel_id=1, source_target_pairs={{0,16},{16,0},{32,48},{48,32},{64,80},{80,64},{96,112},{112,96},{1... | collective-permute-start | bytes 393224 | tf_op jit(solution)/shard_map/ppermute | solution.py:312
  21.2 3.8 %collective-permute-start.6 = (bf16[4,128,128]{2,1,0:T(8,128)(2,1)S(1)}, bf16[4,128,128]{2,1,0:T(8,128)(2,1)S(1)}, u32[]{:S(2)}, u32[]{:S(2)}) collective-permute-start(bf16[4,128,128]{2,1,0:T(8,128)(2,1)S(1)} %get-tuple-element.25), channel_id=1, source_target_pairs={{16,32},{32,16},{48,64},{64,48},{80,96},{96,80},{112,128},{128,112... | collective-permute-start | bytes 393224 | tf_op jit(solution)/shard_map/ppermute | solution.py:315
  24.9 0.3 collective-permute-done.refs_0_.refs_1_.one_r
  25.2 1.2 %collective-permute-done.1.refs_1_.refs_2_.three_r = bf16[8,64,128]{2,1,0:T(8,128)(2,1)S(1)} collective-permute-done((bf16[8,64,128]{2,1,0:T(8,128)(2,1)S(1)}, bf16[8,64,128]{2,1,0:T(8,128)(2,1)S(1)}, u32[]{:S(2)}, u32[]{:S(2)}) %collective-permute-start.1) | collective-permute-done | bytes 131104 | tf_op jit(solution)/shard_map/ppermute | solution.py:309
  26.5 3.4 %collective-permute-start.2 = (bf16[4,128,128]{2,1,0:T(8,128)(2,1)S(1)}, bf16[4,128,128]{2,1,0:T(8,128)(2,1)S(1)}, u32[]{:S(2)}, u32[]{:S(2)}) collective-permute-start(bf16[4,128,128]{2,1,0:T(8,128)(2,1)S(1)} %get-tuple-element.21), channel_id=1, source_target_pairs={{0,16},{16,0},{32,48},{48,32},{64,80},{80,64},{96,112},{112,96},{1... | collective-permute-start | bytes 393224 | tf_op jit(solution)/shard_map/ppermute | solution.py:312
  29.9 3.8 %collective-permute-start.3 = (bf16[4,128,128]{2,1,0:T(8,128)(2,1)S(1)}, bf16[4,128,128]{2,1,0:T(8,128)(2,1)S(1)}, u32[]{:S(2)}, u32[]{:S(2)}) collective-permute-start(bf16[4,128,128]{2,1,0:T(8,128)(2,1)S(1)} %get-tuple-element.22), channel_id=1, source_target_pairs={{16,32},{32,16},{48,64},{64,48},{80,96},{96,80},{112,128},{128,112... | collective-permute-start | bytes 393224 | tf_op jit(solution)/shard_map/ppermute | solution.py:315
  33.6 0.0 copy-start.3
  33.6 0.0 copy-start.4
  33.6 0.0 copy-done.2
  33.7 0.0 copy-done.1
  33.7 0.6 %copy-done.3 = f32[64]{0:T(128)S(1)} copy-done((f32[64]{0:T(128)S(1)}, f32[64]{0:T(128)}, u32[]{:S(2)}) %copy-start.3) | copy-done | bytes 280
  34.3 0.0 copy-done.4
  34.3 0.2 weights.1
  34.5 0.0 collective-permute-done.5.near_r
  34.5 0.0 collective-permute-done.6.far_r
  34.5 1.0 %merge_own.1.refs_3_.mine_r = bf16[12,64,128]{2,1,0:T(8,128)(2,1)S(1)} custom-call(bf16[4,128,128]{2,1,0:T(8,128)(2,1)S(1)} %collective-permute-done.5.near_r, bf16[4,128,128]{2,1,0:T(8,128)(2,1)S(1)} %collective-permute-done.6.far_r, bf16[8,64,128]{2,1,0:T(8,128)(2,1)S(1)} %get-tuple-element.23.refs_0_.own_r, ...), custom_call_target="tpu_custom_call" | custom-call | tf_op jit(solution)/shard_map/merge_own/pallas_call | solution.py:203
  35.5 0.0 collective-permute-done.2.refs_0_.near_r
  35.5 1.5 %merge_inner.1 = (bf16[2,64,128]{2,1,0:T(8,128)(2,1)S(1)}, bf16[2,128,128]{2,1,0:T(8,128)(2,1)S(1)}, bf16[2,64,128]{2,1,0:T(8,128)(2,1)S(1)}, f32[4,64,128]{2,1,0:T(8,128)S(1)}) custom-call(bf16[4,128,128]{2,1,0:T(8,128)(2,1)S(1)} %collective-permute-done.2.refs_0_.near_r, bf16[8,64,128]{2,1,0:T(8,128)(2,1)S(1)} %collective-permute-done.refs_0_.refs_1_.one_r, ...), custom_call_target="tpu_custom_call" | custom-call | tf_op jit(solution)/shard_map/merge_inner/pallas_call | solution.py:234
  37.0 2.8 %collective-permute-done.3.far_r = bf16[4,128,128]{2,1,0:T(8,128)(2,1)S(1)} collective-permute-done((bf16[4,128,128]{2,1,0:T(8,128)(2,1)S(1)}, bf16[4,128,128]{2,1,0:T(8,128)(2,1)S(1)}, u32[]{:S(2)}, u32[]{:S(2)}) %collective-permute-start.3) | collective-permute-done | bytes 131104 | tf_op jit(solution)/shard_map/ppermute | solution.py:315
  39.8 2.0 %merge_outer.1 = bf16[64,8,128]{2,1,0:T(8,128)(2,1)} custom-call(bf16[4,128,128]{2,1,0:T(8,128)(2,1)S(1)} %collective-permute-done.2.refs_0_.near_r, bf16[4,128,128]{2,1,0:T(8,128)(2,1)S(1)} %collective-permute-done.3.far_r, bf16[8,64,128]{2,1,0:T(8,128)(2,1)S(1)} %collective-permute-done.refs_0_.refs_1_.one_r, ...), custom_call_target="tpu_custom_call" | custom-call | tf_op jit(solution)/shard_map/merge_outer/pallas_call | solution.py:286
  (2 shorter events, 0.0 us)
Async XLA Ops:
  0.0 11.7 %copy-start = (bf16[4,64,8,128]{3,2,1,0:T(8,128)(2,1)S(1)}, bf16[4,64,8,128]{3,2,1,0:T(8,128)(2,1)}, u32[]{:S(2)}) copy-start(bf16[4,64,8,128]{3,2,1,0:T(8,128)(2,1)} %src.3) | copy-start | bytes 1572868
  1.0 16.8 %collective-permute-start.4 = (bf16[8,64,128]{2,1,0:T(8,128)(2,1)S(1)}, bf16[8,64,128]{2,1,0:T(8,128)(2,1)S(1)}, u32[]{:S(2)}, u32[]{:S(2)}) collective-permute-start(bf16[8,64,128]{2,1,0:T(8,128)(2,1)S(1)} %lead.1), channel_id=1, source_target_pairs={{0,8},{1,9},{2,10},{3,11},{4,12},{5,13},{6,14},{7,15},{8,0},{9,1},... | collective-permute-start | bytes 393224 | tf_op jit(solution)/shard_map/ppermute | solution.py:309
  11.9 13.3 %collective-permute-start = (bf16[8,64,128]{2,1,0:T(8,128)(2,1)S(1)}, bf16[8,64,128]{2,1,0:T(8,128)(2,1)S(1)}, u32[]{:S(2)}, u32[]{:S(2)}) collective-permute-start(bf16[8,64,128]{2,1,0:T(8,128)(2,1)S(1)} %get-tuple-element.19), channel_id=1, source_target_pairs={{0,4},{1,5},{2,6},{3,7},{4,0},{5,1},{6,2},{7,3},{8,12},{9,13},{10,... | collective-permute-start | bytes 393224 | tf_op jit(solution)/shard_map/ppermute | solution.py:309
  15.9 10.5 %collective-permute-start.1 = (bf16[8,64,128]{2,1,0:T(8,128)(2,1)S(1)}, bf16[8,64,128]{2,1,0:T(8,128)(2,1)S(1)}, u32[]{:S(2)}, u32[]{:S(2)}) collective-permute-start(bf16[8,64,128]{2,1,0:T(8,128)(2,1)S(1)} %get-tuple-element.20), channel_id=1, source_target_pairs={{0,12},{1,13},{2,14},{3,15},{4,8},{5,9},{6,10},{7,11},{8,4},{9,5},... | collective-permute-start | bytes 393224 | tf_op jit(solution)/shard_map/ppermute | solution.py:309
  17.8 15.8 %copy-start.2 = (bf16[3,3,64,64]{3,2,1,0:T(8,128)(2,1)S(1)}, bf16[3,3,64,64]{3,2,1,0:T(8,128)(2,1)}, u32[]{:S(2)}) copy-start(bf16[3,3,64,64]{3,2,1,0:T(8,128)(2,1)} %param.7) | copy-start | bytes 221188
  17.9 15.8 %copy-start.1 = (bf16[3,3,64,128]{3,2,1,0:T(8,128)(2,1)S(1)}, bf16[3,3,64,128]{3,2,1,0:T(8,128)(2,1)}, u32[]{:S(2)}) copy-start(bf16[3,3,64,128]{3,2,1,0:T(8,128)(2,1)} %param.6) | copy-start | bytes 442372
  17.9 16.6 %collective-permute-start.5 = (bf16[4,128,128]{2,1,0:T(8,128)(2,1)S(1)}, bf16[4,128,128]{2,1,0:T(8,128)(2,1)S(1)}, u32[]{:S(2)}, u32[]{:S(2)}) collective-permute-start(bf16[4,128,128]{2,1,0:T(8,128)(2,1)S(1)} %get-tuple-element.24), channel_id=1, source_target_pairs={{0,16},{16,0},{32,48},{48,32},{64,80},{80,64},{96,112},{112,96},{1... | collective-permute-start | bytes 393224 | tf_op jit(solution)/shard_map/ppermute | solution.py:312
  21.2 13.3 %collective-permute-start.6 = (bf16[4,128,128]{2,1,0:T(8,128)(2,1)S(1)}, bf16[4,128,128]{2,1,0:T(8,128)(2,1)S(1)}, u32[]{:S(2)}, u32[]{:S(2)}) collective-permute-start(bf16[4,128,128]{2,1,0:T(8,128)(2,1)S(1)} %get-tuple-element.25), channel_id=1, source_target_pairs={{16,32},{32,16},{48,64},{64,48},{80,96},{96,80},{112,128},{128,112... | collective-permute-start | bytes 393224 | tf_op jit(solution)/shard_map/ppermute | solution.py:315
  26.5 9.0 %collective-permute-start.2 = (bf16[4,128,128]{2,1,0:T(8,128)(2,1)S(1)}, bf16[4,128,128]{2,1,0:T(8,128)(2,1)S(1)}, u32[]{:S(2)}, u32[]{:S(2)}) collective-permute-start(bf16[4,128,128]{2,1,0:T(8,128)(2,1)S(1)} %get-tuple-element.21), channel_id=1, source_target_pairs={{0,16},{16,0},{32,48},{48,32},{64,80},{80,64},{96,112},{112,96},{1... | collective-permute-start | bytes 393224 | tf_op jit(solution)/shard_map/ppermute | solution.py:312
  29.9 9.9 %collective-permute-start.3 = (bf16[4,128,128]{2,1,0:T(8,128)(2,1)S(1)}, bf16[4,128,128]{2,1,0:T(8,128)(2,1)S(1)}, u32[]{:S(2)}, u32[]{:S(2)}) collective-permute-start(bf16[4,128,128]{2,1,0:T(8,128)(2,1)S(1)} %get-tuple-element.22), channel_id=1, source_target_pairs={{16,32},{32,16},{48,64},{64,48},{80,96},{96,80},{112,128},{128,112... | collective-permute-start | bytes 393224 | tf_op jit(solution)/shard_map/ppermute | solution.py:315
  33.6 0.7 %copy-start.3 = (f32[64]{0:T(128)S(1)}, f32[64]{0:T(128)}, u32[]{:S(2)}) copy-start(f32[64]{0:T(128)} %param.8) | copy-start | bytes 772
  33.6 0.7 %copy-start.4 = (f32[64]{0:T(128)S(1)}, f32[64]{0:T(128)}, u32[]{:S(2)}) copy-start(f32[64]{0:T(128)} %param.9) | copy-start | bytes 772

commit v5 on v4

--- a/solution.py
+++ b/solution.py
@@ -81,8 +81,8 @@
     )(frames)
 
 
-def weights(w_pair, w_mixed, slope_pair, slope_mixed):
-    def body(wp, wm, sp, sm, pair, mixed, cols):
+def weights(w_pair, w_mixed):
+    def body(wp, wm, pair, mixed):
         top = 2 - 2 * odd_row()
         taps = (top, 1, 2 - top)
         for ky in range(3):
@@ -91,19 +91,15 @@
             pair[0, :, at : at + 2 * CH] = tap
             pair[1, :, at : at + 2 * CH] = jnp.concatenate([tap[:, CH:], tap[:, :CH]], axis=1)
         mixed[...] = jnp.concatenate([wm[taps[0]], wm[1], wm[taps[2]]], axis=1)
-        square = lax.broadcasted_iota(jnp.int32, (CH, CH), 0) == lax.broadcasted_iota(jnp.int32, (CH, CH), 1)
-        for k, slope in enumerate((sp, sm)):
-            column = jnp.sum(jnp.where(square, slope[...], 0.0), axis=1, keepdims=True)
-            cols[k] = jnp.broadcast_to(column, (CH, LANES))
-
-    return pl.pallas_call(
-        body,
-        out_shape=(array(2, 3 * CH, 6 * CH), array(3 * CH, 3 * CH), array(2, CH, LANES, dtype=jnp.float32)),
-        in_specs=[VMEM] * 4,
-        out_specs=(VMEM,) * 3,
+
+    return pl.pallas_call(
+        body,
+        out_shape=(array(2, 3 * CH, 6 * CH), array(3 * CH, 3 * CH)),
+        in_specs=[VMEM] * 2,
+        out_specs=(VMEM,) * 2,
         compiler_params=SMALL,
         name="weights",
-    )(w_pair.reshape(3, 3 * CH, 2 * CH), w_mixed.reshape(3, 3 * CH, CH), slope_pair.reshape(1, CH), slope_mixed.reshape(1, CH))
+    )(w_pair.reshape(3, 3 * CH, 2 * CH), w_mixed.reshape(3, 3 * CH, CH))
 
 
 def edges(*frames):
@@ -137,13 +133,17 @@
 
 
 class Level:
-    def __init__(self, pair, mixed, cols, swap, hid):
+    def __init__(self, pair, mixed, sp, sm, swap, hid):
         lane = lax.broadcasted_iota(jnp.int32, (CH, LANES), 1)
         self.not_first = lane > 0
         self.not_last = lane < LANES - 1
         self.pair = pair[swap]
         self.mixed = mixed[...]
-        self.cols = cols
+        square = lax.broadcasted_iota(jnp.int32, (CH, CH), 0) == lax.broadcasted_iota(jnp.int32, (CH, CH), 1)
+        self.cols = [
+            jnp.broadcast_to(jnp.sum(jnp.where(square, slope[...], 0.0), axis=1, keepdims=True), (CH, LANES))
+            for slope in (sp, sm)
+        ]
         self.swap = swap
         self.hid = hid
         place = lax.axis_index("row")
@@ -191,19 +191,19 @@
 
 
 def merge_own(near_side, far_side, own, two, tables):
-    def body(near_r, far_r, own_r, two_r, pair, mixed, cols, out, stack, hid):
+    def body(near_r, far_r, own_r, two_r, pair, mixed, sp, sm, out, stack, hid):
         for slot, frame in enumerate((own_r, two_r)):
             fill(stack, slot, near_r, 0, slot)
             fill(stack, slot, frame, HALO)
             fill(stack, slot, far_r, HALO + ROWS, slot)
-        level = Level(pair, mixed, cols, position() // 2, hid)
+        level = Level(pair, mixed, sp, sm, position() // 2, hid)
         level.first(stack, 0, 1, 15)
         level.second(stack, 0, 2, 14, into(out, 2, slice(None)))
 
     return pl.pallas_call(
         body,
         out_shape=array(12, CH, LANES),
-        in_specs=[VMEM] * 7,
+        in_specs=[VMEM] * 8,
         out_specs=VMEM,
         scratch_shapes=[STACK, HIDDEN],
         compiler_params=SMALL,
@@ -215,16 +215,16 @@
     def body(*refs):
         pl.when(at_seam())(partial(inner, *refs))
 
-    def inner(near_r, one_r, three_r, mine_r, pair, mixed, cols, hid_end, ones_end, top_end, done, stack, ones, hid, top_hid):
+    def inner(near_r, one_r, three_r, mine_r, pair, mixed, sp, sm, hid_end, ones_end, top_end, done, stack, ones, hid, top_hid):
         for slot, frame in enumerate((one_r, three_r)):
             fill(stack, slot, near_r, 0, slot)
             fill(stack, slot, frame, HALO)
         fill(ones, 0, mine_r.at[0:8], 2)
         at = position()
-        level = Level(pair, mixed, cols, at // 2, hid)
+        level = Level(pair, mixed, sp, sm, at // 2, hid)
         level.first(stack, 0, 1, 11)
         level.second(stack, 0, 2, 10, into(ones, 0, OTHER))
-        top = Level(pair, mixed, cols, at % 2, top_hid)
+        top = Level(pair, mixed, sp, sm, at % 2, top_hid)
         top.first(ones, 0, 3, 9)
         top.second(ones, 0, 4, 8, into(done, 4, slice(None)))
         hid_end[...] = hid[9:11]
@@ -234,7 +234,7 @@
     return pl.pallas_call(
         body,
         out_shape=(array(2, CH, LANES), array(2, 2 * CH, LANES), array(2, CH, LANES), array(4, CH, LANES, dtype=jnp.float32)),
-        in_specs=[VMEM] * 7,
+        in_specs=[VMEM] * 8,
         out_specs=(VMEM,) * 4,
         scratch_shapes=[STACK, STACK, HIDDEN, HIDDEN],
         compiler_params=SMALL,
@@ -243,7 +243,7 @@
 
 
 def merge_outer(near_side, far_side, one, three, mine, inner, tables):
-    def body(near_r, far_r, one_r, three_r, mine_r, hid_end, ones_end, top_end, done, pair, mixed, cols, out, stack, ones, hid, top_hid, rows, wide):
+    def body(near_r, far_r, one_r, three_r, mine_r, hid_end, ones_end, top_end, done, pair, mixed, sp, sm, out, stack, ones, hid, top_hid, rows, wide):
         at = position()
 
         @pl.when(at_seam())
@@ -256,10 +256,10 @@
             fill(ones, 0, mine_r.at[8:12], 10)
             top_hid[7:9] = top_end[...]
             rows[0:4] = done[...]
-            level = Level(pair, mixed, cols, at // 2, hid)
+            level = Level(pair, mixed, sp, sm, at // 2, hid)
             level.first(stack, 0, 11, 15)
             level.second(stack, 0, 10, 14, into(ones, 0, OTHER))
-            top = Level(pair, mixed, cols, at % 2, top_hid)
+            top = Level(pair, mixed, sp, sm, at % 2, top_hid)
             top.first(ones, 0, 9, 13)
             top.second(ones, 0, 8, 12, into(rows, 4, slice(None)))
 
@@ -270,10 +270,10 @@
                 fill(stack, slot, frame, HALO)
                 fill(stack, slot, far_r, HALO + ROWS, slot)
             fill(ones, 0, mine_r, 2)
-            level = Level(pair, mixed, cols, at // 2, hid)
+            level = Level(pair, mixed, sp, sm, at // 2, hid)
             level.first(stack, 0, 1, 15)
             level.second(stack, 0, 2, 14, into(ones, 0, OTHER))
-            top = Level(pair, mixed, cols, at % 2, top_hid)
+            top = Level(pair, mixed, sp, sm, at % 2, top_hid)
             top.first(ones, 0, 3, 13)
             top.second(ones, 0, 4, 12, into(rows, 4, slice(None)))
 
@@ -286,7 +286,7 @@
     return pl.pallas_call(
         body,
         out_shape=array(CH, ROWS, LANES),
-        in_specs=[VMEM] * 12,
+        in_specs=[VMEM] * 13,
         scratch_shapes=[
             STACK,
             STACK,
@@ -319,7 +319,7 @@
     one = swapped(one, 1)
     three = swapped(three, 3)
     two = swapped(two, 2)
-    tables = weights(w_pair, w_mixed, slope_pair, slope_mixed)
+    tables = (*weights(w_pair, w_mixed), slope_pair.reshape(1, CH), slope_mixed.reshape(1, CH))
     near_early, far_early = edges(own, two)
     far_early = off_chip(far_early)
     near_early = on_chip(near_early)

time: 42.1 us -> 42.1 us (level)
  no operation moved by 1% of the time
where the time goes in v5:
time: 42.1 us; the launch traced here: 41.7 us
  starting transfers between devices  30.7 us (73%)
  Pallas kernels  5.83 us (14%)
  waiting for transfers between devices  4.31 us (10%)
  local copies, waits for them, and re-layouts  0.67 us (2%)
    ppermute x3, starting transfers between devices, swapped(): lax.ppermute(block, 'frame', [(i, i ^ mask * quarter) for i in range(coun...  16.6 us
    ppermute x2, starting transfers between devices, off_chip(): lax.ppermute(block, 'row', [(i, (i + 1 ^ 1) - 1) for i in range(1, rows -...  7.51 us
    ppermute x2, starting transfers between devices, on_chip(): return lax.ppermute(block, 'row', [(i, i ^ 1) for i in range(rows)])  6.66 us
    ppermute x2, waiting for transfers between devices, off_chip(): lax.ppermute(block, 'row', [(i, (i + 1 ^ 1) - 1) for i in range(1, rows -...  2.8 us
    pallas_call x1, Pallas kernels, merge_outer(): pl.pallas_call(body, out_shape=array(CH, ROWS, LANES), in_specs=[VMEM] *...  1.98 us
    ppermute x3, waiting for transfers between devices, swapped(): lax.ppermute(block, 'frame', [(i, i ^ mask * quarter) for i in range(coun...  1.5 us
    pallas_call x1, Pallas kernels, merge_inner(): pl.pallas_call(body, out_shape=(array(2, CH, LANES), array(2, 2 * CH, LAN...  1.49 us
    pallas_call x1, Pallas kernels, lead(): pl.pallas_call(body, out_shape=array(ROWS, CH, LANES), in_specs=[pl.Block...  1.02 us
  transfers between devices with their start and end apart: 7, of which 3 were waited for; matrix products, arithmetic and copies ran while one was open for 0% of the time, Pallas kernels for 7%

profile of v5, /device:TPU:57, one launch (start us, length us, event | category | flops | bytes accessed | tf_op | source)
XLA Modules:
  0.0 41.7 jit_solution(14301291945396993399)
XLA Ops:
  0.0 0.0 copy-start
  0.0 1.0 %lead.1 = bf16[8,64,128]{2,1,0:T(8,128)(2,1)S(1)} custom-call(bf16[4,64,8,128]{3,2,1,0:T(8,128)(2,1)} %src.3), custom_call_target="tpu_custom_call" | custom-call | tf_op jit(solution)/shard_map/lead/pallas_call | solution.py:44
  1.0 10.6 %collective-permute-start.4 = (bf16[8,64,128]{2,1,0:T(8,128)(2,1)S(1)}, bf16[8,64,128]{2,1,0:T(8,128)(2,1)S(1)}, u32[]{:S(2)}, u32[]{:S(2)}) collective-permute-start(bf16[8,64,128]{2,1,0:T(8,128)(2,1)S(1)} %lead.1), channel_id=1, source_target_pairs={{0,8},{1,9},{2,10},{3,11},{4,12},{5,13},{6,14},{7,15},{8,0},{9,1},... | collective-permute-start | bytes 393224 | tf_op jit(solution)/shard_map/ppermute | solution.py:309
  11.7 0.0 copy-done
  11.7 0.2 spread.1
  11.9 4.0 %collective-permute-start = (bf16[8,64,128]{2,1,0:T(8,128)(2,1)S(1)}, bf16[8,64,128]{2,1,0:T(8,128)(2,1)S(1)}, u32[]{:S(2)}, u32[]{:S(2)}) collective-permute-start(bf16[8,64,128]{2,1,0:T(8,128)(2,1)S(1)} %get-tuple-element.18), channel_id=1, source_target_pairs={{0,4},{1,5},{2,6},{3,7},{4,0},{5,1},{6,2},{7,3},{8,12},{9,13},{10,... | collective-permute-start | bytes 393224 | tf_op jit(solution)/shard_map/ppermute | solution.py:309
  15.9 1.9 %collective-permute-start.1 = (bf16[8,64,128]{2,1,0:T(8,128)(2,1)S(1)}, bf16[8,64,128]{2,1,0:T(8,128)(2,1)S(1)}, u32[]{:S(2)}, u32[]{:S(2)}) collective-permute-start(bf16[8,64,128]{2,1,0:T(8,128)(2,1)S(1)} %get-tuple-element.19), channel_id=1, source_target_pairs={{0,12},{1,13},{2,14},{3,15},{4,8},{5,9},{6,10},{7,11},{8,4},{9,5},... | collective-permute-start | bytes 393224 | tf_op jit(solution)/shard_map/ppermute | solution.py:309
  17.8 0.0 collective-permute-done.4.refs_1_.two_r
  17.8 0.0 copy-start.2
  17.9 0.0 copy-start.1
  17.9 3.3 %collective-permute-start.5 = (bf16[4,128,128]{2,1,0:T(8,128)(2,1)S(1)}, bf16[4,128,128]{2,1,0:T(8,128)(2,1)S(1)}, u32[]{:S(2)}, u32[]{:S(2)}) collective-permute-start(bf16[4,128,128]{2,1,0:T(8,128)(2,1)S(1)} %get-tuple-element.23), channel_id=1, source_target_pairs={{0,16},{16,0},{32,48},{48,32},{64,80},{80,64},{96,112},{112,96},{1... | collective-permute-start | bytes 393224 | tf_op jit(solution)/shard_map/ppermute | solution.py:312
  21.2 3.8 %collective-permute-start.6 = (bf16[4,128,128]{2,1,0:T(8,128)(2,1)S(1)}, bf16[4,128,128]{2,1,0:T(8,128)(2,1)S(1)}, u32[]{:S(2)}, u32[]{:S(2)}) collective-permute-start(bf16[4,128,128]{2,1,0:T(8,128)(2,1)S(1)} %get-tuple-element.24), channel_id=1, source_target_pairs={{16,32},{32,16},{48,64},{64,48},{80,96},{96,80},{112,128},{128,112... | collective-permute-start | bytes 393224 | tf_op jit(solution)/shard_map/ppermute | solution.py:315
  24.9 0.3 collective-permute-done.refs_0_.refs_1_.one_r
  25.2 1.2 %collective-permute-done.1.refs_1_.refs_2_.three_r = bf16[8,64,128]{2,1,0:T(8,128)(2,1)S(1)} collective-permute-done((bf16[8,64,128]{2,1,0:T(8,128)(2,1)S(1)}, bf16[8,64,128]{2,1,0:T(8,128)(2,1)S(1)}, u32[]{:S(2)}, u32[]{:S(2)}) %collective-permute-start.1) | collective-permute-done | bytes 131104 | tf_op jit(solution)/shard_map/ppermute | solution.py:309
  26.5 3.4 %collective-permute-start.2 = (bf16[4,128,128]{2,1,0:T(8,128)(2,1)S(1)}, bf16[4,128,128]{2,1,0:T(8,128)(2,1)S(1)}, u32[]{:S(2)}, u32[]{:S(2)}) collective-permute-start(bf16[4,128,128]{2,1,0:T(8,128)(2,1)S(1)} %get-tuple-element.20), channel_id=1, source_target_pairs={{0,16},{16,0},{32,48},{48,32},{64,80},{80,64},{96,112},{112,96},{1... | collective-permute-start | bytes 393224 | tf_op jit(solution)/shard_map/ppermute | solution.py:312
  29.9 3.8 %collective-permute-start.3 = (bf16[4,128,128]{2,1,0:T(8,128)(2,1)S(1)}, bf16[4,128,128]{2,1,0:T(8,128)(2,1)S(1)}, u32[]{:S(2)}, u32[]{:S(2)}) collective-permute-start(bf16[4,128,128]{2,1,0:T(8,128)(2,1)S(1)} %get-tuple-element.21), channel_id=1, source_target_pairs={{16,32},{32,16},{48,64},{64,48},{80,96},{96,80},{112,128},{128,112... | collective-permute-start | bytes 393224 | tf_op jit(solution)/shard_map/ppermute | solution.py:315
  33.6 0.0 copy-done.2
  33.6 0.0 copy-done.1
  33.6 0.1 weights.1
  33.8 0.0 collective-permute-done.5.near_r
  33.8 0.0 collective-permute-done.6.far_r
  33.8 0.0 copy-start.3
  33.8 0.0 copy-start.4
  33.8 0.6 %copy-done.3 = f32[64]{0:T(128)S(1)} copy-done((f32[64]{0:T(128)S(1)}, f32[64]{0:T(128)}, u32[]{:S(2)}) %copy-start.3) | copy-done | bytes 280
  34.5 0.0 copy-done.4
  34.5 1.0 %merge_own.1.refs_3_.mine_r = bf16[12,64,128]{2,1,0:T(8,128)(2,1)S(1)} custom-call(bf16[4,128,128]{2,1,0:T(8,128)(2,1)S(1)} %collective-permute-done.5.near_r, bf16[4,128,128]{2,1,0:T(8,128)(2,1)S(1)} %collective-permute-done.6.far_r, bf16[8,64,128]{2,1,0:T(8,128)(2,1)S(1)} %get-tuple-element.22.refs_0_.own_r, ...), custom_call_target="tpu_custom_call" | custom-call | tf_op jit(solution)/shard_map/merge_own/pallas_call | solution.py:203
  35.5 0.0 collective-permute-done.2.refs_0_.near_r
  35.5 1.5 %merge_inner.1 = (bf16[2,64,128]{2,1,0:T(8,128)(2,1)S(1)}, bf16[2,128,128]{2,1,0:T(8,128)(2,1)S(1)}, bf16[2,64,128]{2,1,0:T(8,128)(2,1)S(1)}, f32[4,64,128]{2,1,0:T(8,128)S(1)}) custom-call(bf16[4,128,128]{2,1,0:T(8,128)(2,1)S(1)} %collective-permute-done.2.refs_0_.near_r, bf16[8,64,128]{2,1,0:T(8,128)(2,1)S(1)} %collective-permute-done.refs_0_.refs_1_.one_r, ...), custom_call_target="tpu_custom_call" | custom-call | tf_op jit(solution)/shard_map/merge_inner/pallas_call | solution.py:234
  37.0 2.8 %collective-permute-done.3.far_r = bf16[4,128,128]{2,1,0:T(8,128)(2,1)S(1)} collective-permute-done((bf16[4,128,128]{2,1,0:T(8,128)(2,1)S(1)}, bf16[4,128,128]{2,1,0:T(8,128)(2,1)S(1)}, u32[]{:S(2)}, u32[]{:S(2)}) %collective-permute-start.3) | collective-permute-done | bytes 131104 | tf_op jit(solution)/shard_map/ppermute | solution.py:315
  39.8 2.0 %merge_outer.1 = bf16[64,8,128]{2,1,0:T(8,128)(2,1)} custom-call(bf16[4,128,128]{2,1,0:T(8,128)(2,1)S(1)} %collective-permute-done.2.refs_0_.near_r, bf16[4,128,128]{2,1,0:T(8,128)(2,1)S(1)} %collective-permute-done.3.far_r, bf16[8,64,128]{2,1,0:T(8,128)(2,1)S(1)} %collective-permute-done.refs_0_.refs_1_.one_r, ...), custom_call_target="tpu_custom_call" | custom-call | tf_op jit(solution)/shard_map/merge_outer/pallas_call | solution.py:286
  (2 shorter events, 0.0 us)
Async XLA Ops:
  0.0 11.7 %copy-start = (bf16[4,64,8,128]{3,2,1,0:T(8,128)(2,1)S(1)}, bf16[4,64,8,128]{3,2,1,0:T(8,128)(2,1)}, u32[]{:S(2)}) copy-start(bf16[4,64,8,128]{3,2,1,0:T(8,128)(2,1)} %src.3) | copy-start | bytes 1572868
  1.0 16.8 %collective-permute-start.4 = (bf16[8,64,128]{2,1,0:T(8,128)(2,1)S(1)}, bf16[8,64,128]{2,1,0:T(8,128)(2,1)S(1)}, u32[]{:S(2)}, u32[]{:S(2)}) collective-permute-start(bf16[8,64,128]{2,1,0:T(8,128)(2,1)S(1)} %lead.1), channel_id=1, source_target_pairs={{0,8},{1,9},{2,10},{3,11},{4,12},{5,13},{6,14},{7,15},{8,0},{9,1},... | collective-permute-start | bytes 393224 | tf_op jit(solution)/shard_map/ppermute | solution.py:309
  11.9 13.3 %collective-permute-start = (bf16[8,64,128]{2,1,0:T(8,128)(2,1)S(1)}, bf16[8,64,128]{2,1,0:T(8,128)(2,1)S(1)}, u32[]{:S(2)}, u32[]{:S(2)}) collective-permute-start(bf16[8,64,128]{2,1,0:T(8,128)(2,1)S(1)} %get-tuple-element.18), channel_id=1, source_target_pairs={{0,4},{1,5},{2,6},{3,7},{4,0},{5,1},{6,2},{7,3},{8,12},{9,13},{10,... | collective-permute-start | bytes 393224 | tf_op jit(solution)/shard_map/ppermute | solution.py:309
  15.9 10.5 %collective-permute-start.1 = (bf16[8,64,128]{2,1,0:T(8,128)(2,1)S(1)}, bf16[8,64,128]{2,1,0:T(8,128)(2,1)S(1)}, u32[]{:S(2)}, u32[]{:S(2)}) collective-permute-start(bf16[8,64,128]{2,1,0:T(8,128)(2,1)S(1)} %get-tuple-element.19), channel_id=1, source_target_pairs={{0,12},{1,13},{2,14},{3,15},{4,8},{5,9},{6,10},{7,11},{8,4},{9,5},... | collective-permute-start | bytes 393224 | tf_op jit(solution)/shard_map/ppermute | solution.py:309
  17.8 15.8 %copy-start.2 = (bf16[3,3,64,64]{3,2,1,0:T(8,128)(2,1)S(1)}, bf16[3,3,64,64]{3,2,1,0:T(8,128)(2,1)}, u32[]{:S(2)}) copy-start(bf16[3,3,64,64]{3,2,1,0:T(8,128)(2,1)} %param.7) | copy-start | bytes 221188
  17.9 15.7 %copy-start.1 = (bf16[3,3,64,128]{3,2,1,0:T(8,128)(2,1)S(1)}, bf16[3,3,64,128]{3,2,1,0:T(8,128)(2,1)}, u32[]{:S(2)}) copy-start(bf16[3,3,64,128]{3,2,1,0:T(8,128)(2,1)} %param.6) | copy-start | bytes 442372
  17.9 15.9 %collective-permute-start.5 = (bf16[4,128,128]{2,1,0:T(8,128)(2,1)S(1)}, bf16[4,128,128]{2,1,0:T(8,128)(2,1)S(1)}, u32[]{:S(2)}, u32[]{:S(2)}) collective-permute-start(bf16[4,128,128]{2,1,0:T(8,128)(2,1)S(1)} %get-tuple-element.23), channel_id=1, source_target_pairs={{0,16},{16,0},{32,48},{48,32},{64,80},{80,64},{96,112},{112,96},{1... | collective-permute-start | bytes 393224 | tf_op jit(solution)/shard_map/ppermute | solution.py:312
  21.2 12.6 %collective-permute-start.6 = (bf16[4,128,128]{2,1,0:T(8,128)(2,1)S(1)}, bf16[4,128,128]{2,1,0:T(8,128)(2,1)S(1)}, u32[]{:S(2)}, u32[]{:S(2)}) collective-permute-start(bf16[4,128,128]{2,1,0:T(8,128)(2,1)S(1)} %get-tuple-element.24), channel_id=1, source_target_pairs={{16,32},{32,16},{48,64},{64,48},{80,96},{96,80},{112,128},{128,112... | collective-permute-start | bytes 393224 | tf_op jit(solution)/shard_map/ppermute | solution.py:315
  26.5 9.0 %collective-permute-start.2 = (bf16[4,128,128]{2,1,0:T(8,128)(2,1)S(1)}, bf16[4,128,128]{2,1,0:T(8,128)(2,1)S(1)}, u32[]{:S(2)}, u32[]{:S(2)}) collective-permute-start(bf16[4,128,128]{2,1,0:T(8,128)(2,1)S(1)} %get-tuple-element.20), channel_id=1, source_target_pairs={{0,16},{16,0},{32,48},{48,32},{64,80},{80,64},{96,112},{112,96},{1... | collective-permute-start | bytes 393224 | tf_op jit(solution)/shard_map/ppermute | solution.py:312
  29.9 9.9 %collective-permute-start.3 = (bf16[4,128,128]{2,1,0:T(8,128)(2,1)S(1)}, bf16[4,128,128]{2,1,0:T(8,128)(2,1)S(1)}, u32[]{:S(2)}, u32[]{:S(2)}) collective-permute-start(bf16[4,128,128]{2,1,0:T(8,128)(2,1)S(1)} %get-tuple-element.21), channel_id=1, source_target_pairs={{16,32},{32,16},{48,64},{64,48},{80,96},{96,80},{112,128},{128,112... | collective-permute-start | bytes 393224 | tf_op jit(solution)/shard_map/ppermute | solution.py:315
  33.8 0.7 %copy-start.3 = (f32[64]{0:T(128)S(1)}, f32[64]{0:T(128)}, u32[]{:S(2)}) copy-start(f32[64]{0:T(128)} %param.8) | copy-start | bytes 772
  33.8 0.7 %copy-start.4 = (f32[64]{0:T(128)S(1)}, f32[64]{0:T(128)}, u32[]{:S(2)}) copy-start(f32[64]{0:T(128)} %param.9) | copy-start | bytes 772

commit v6 on v5

--- a/solution.py
+++ b/solution.py
@@ -132,18 +132,22 @@
     return (row == half) | (row == half - 1)
 
 
+def columns(*slopes):
+    square = lax.broadcasted_iota(jnp.int32, (CH, CH), 0) == lax.broadcasted_iota(jnp.int32, (CH, CH), 1)
+    return [
+        jnp.broadcast_to(jnp.sum(jnp.where(square, slope[...], 0.0), axis=1, keepdims=True), (CH, LANES))
+        for slope in slopes
+    ]
+
+
 class Level:
-    def __init__(self, pair, mixed, sp, sm, swap, hid):
+    def __init__(self, pair, mixed, cols, swap, hid):
         lane = lax.broadcasted_iota(jnp.int32, (CH, LANES), 1)
         self.not_first = lane > 0
         self.not_last = lane < LANES - 1
         self.pair = pair[swap]
         self.mixed = mixed[...]
-        square = lax.broadcasted_iota(jnp.int32, (CH, CH), 0) == lax.broadcasted_iota(jnp.int32, (CH, CH), 1)
-        self.cols = [
-            jnp.broadcast_to(jnp.sum(jnp.where(square, slope[...], 0.0), axis=1, keepdims=True), (CH, LANES))
-            for slope in (sp, sm)
-        ]
+        self.cols = cols
         self.swap = swap
         self.hid = hid
         place = lax.axis_index("row")
@@ -196,7 +200,8 @@
             fill(stack, slot, near_r, 0, slot)
             fill(stack, slot, frame, HALO)
             fill(stack, slot, far_r, HALO + ROWS, slot)
-        level = Level(pair, mixed, sp, sm, position() // 2, hid)
+        cols = columns(sp, sm)
+        level = Level(pair, mixed, cols, position() // 2, hid)
         level.first(stack, 0, 1, 15)
         level.second(stack, 0, 2, 14, into(out, 2, slice(None)))
 
@@ -221,10 +226,11 @@
             fill(stack, slot, frame, HALO)
         fill(ones, 0, mine_r.at[0:8], 2)
         at = position()
-        level = Level(pair, mixed, sp, sm, at // 2, hid)
+        cols = columns(sp, sm)
+        level = Level(pair, mixed, cols, at // 2, hid)
         level.first(stack, 0, 1, 11)
         level.second(stack, 0, 2, 10, into(ones, 0, OTHER))
-        top = Level(pair, mixed, sp, sm, at % 2, top_hid)
+        top = Level(pair, mixed, cols, at % 2, top_hid)
         top.first(ones, 0, 3, 9)
         top.second(ones, 0, 4, 8, into(done, 4, slice(None)))
         hid_end[...] = hid[9:11]
@@ -256,10 +262,11 @@
             fill(ones, 0, mine_r.at[8:12], 10)
             top_hid[7:9] = top_end[...]
             rows[0:4] = done[...]
-            level = Level(pair, mixed, sp, sm, at // 2, hid)
+            cols = columns(sp, sm)
+            level = Level(pair, mixed, cols, at // 2, hid)
             level.first(stack, 0, 11, 15)
             level.second(stack, 0, 10, 14, into(ones, 0, OTHER))
-            top = Level(pair, mixed, sp, sm, at % 2, top_hid)
+            top = Level(pair, mixed, cols, at % 2, top_hid)
             top.first(ones, 0, 9, 13)
             top.second(ones, 0, 8, 12, into(rows, 4, slice(None)))
 
@@ -270,10 +277,11 @@
                 fill(stack, slot, frame, HALO)
                 fill(stack, slot, far_r, HALO + ROWS, slot)
             fill(ones, 0, mine_r, 2)
-            level = Level(pair, mixed, sp, sm, at // 2, hid)
+            cols = columns(sp, sm)
+            level = Level(pair, mixed, cols, at // 2, hid)
             level.first(stack, 0, 1, 15)
             level.second(stack, 0, 2, 14, into(ones, 0, OTHER))
-            top = Level(pair, mixed, sp, sm, at % 2, top_hid)
+            top = Level(pair, mixed, cols, at % 2, top_hid)
             top.first(ones, 0, 3, 13)
             top.second(ones, 0, 4, 12, into(rows, 4, slice(None)))
 

time: 42.1 us -> 42.1 us (level)
  no operation moved by 1% of the time
where the time goes in v6:
time: 42.1 us; the launch traced here: 41.7 us
  starting transfers between devices  30.7 us (73%)
  Pallas kernels  5.83 us (14%)
  waiting for transfers between devices  4.31 us (10%)
  local copies, waits for them, and re-layouts  0.67 us (2%)
    ppermute x3, starting transfers between devices, swapped(): lax.ppermute(block, 'frame', [(i, i ^ mask * quarter) for i in range(coun...  16.6 us
    ppermute x2, starting transfers between devices, off_chip(): lax.ppermute(block, 'row', [(i, (i + 1 ^ 1) - 1) for i in range(1, rows -...  7.51 us
    ppermute x2, starting transfers between devices, on_chip(): return lax.ppermute(block, 'row', [(i, i ^ 1) for i in range(rows)])  6.66 us
    ppermute x2, waiting for transfers between devices, off_chip(): lax.ppermute(block, 'row', [(i, (i + 1 ^ 1) - 1) for i in range(1, rows -...  2.8 us
    pallas_call x1, Pallas kernels, merge_outer(): pl.pallas_call(body, out_shape=array(CH, ROWS, LANES), in_specs=[VMEM] *...  1.98 us
    ppermute x3, waiting for transfers between devices, swapped(): lax.ppermute(block, 'frame', [(i, i ^ mask * quarter) for i in range(coun...  1.5 us
    pallas_call x1, Pallas kernels, merge_inner(): pl.pallas_call(body, out_shape=(array(2, CH, LANES), array(2, 2 * CH, LAN...  1.49 us
    pallas_call x1, Pallas kernels, lead(): pl.pallas_call(body, out_shape=array(ROWS, CH, LANES), in_specs=[pl.Block...  1.02 us
  transfers between devices with their start and end apart: 7, of which 3 were waited for; matrix products, arithmetic and copies ran while one was open for 0% of the time, Pallas kernels for 7%

profile of v6, /device:TPU:57, one launch (start us, length us, event | category | flops | bytes accessed | tf_op | source)
XLA Modules:
  0.0 41.7 jit_solution(10517178438862236955)
XLA Ops:
  0.0 0.0 copy-start
  0.0 1.0 %lead.1 = bf16[8,64,128]{2,1,0:T(8,128)(2,1)S(1)} custom-call(bf16[4,64,8,128]{3,2,1,0:T(8,128)(2,1)} %src.3), custom_call_target="tpu_custom_call" | custom-call | tf_op jit(solution)/shard_map/lead/pallas_call | solution.py:44
  1.0 10.6 %collective-permute-start.4 = (bf16[8,64,128]{2,1,0:T(8,128)(2,1)S(1)}, bf16[8,64,128]{2,1,0:T(8,128)(2,1)S(1)}, u32[]{:S(2)}, u32[]{:S(2)}) collective-permute-start(bf16[8,64,128]{2,1,0:T(8,128)(2,1)S(1)} %lead.1), channel_id=1, source_target_pairs={{0,8},{1,9},{2,10},{3,11},{4,12},{5,13},{6,14},{7,15},{8,0},{9,1},... | collective-permute-start | bytes 393224 | tf_op jit(solution)/shard_map/ppermute | solution.py:317
  11.7 0.0 copy-done
  11.7 0.2 spread.1
  11.9 4.0 %collective-permute-start = (bf16[8,64,128]{2,1,0:T(8,128)(2,1)S(1)}, bf16[8,64,128]{2,1,0:T(8,128)(2,1)S(1)}, u32[]{:S(2)}, u32[]{:S(2)}) collective-permute-start(bf16[8,64,128]{2,1,0:T(8,128)(2,1)S(1)} %get-tuple-element.18), channel_id=1, source_target_pairs={{0,4},{1,5},{2,6},{3,7},{4,0},{5,1},{6,2},{7,3},{8,12},{9,13},{10,... | collective-permute-start | bytes 393224 | tf_op jit(solution)/shard_map/ppermute | solution.py:317
  15.9 1.9 %collective-permute-start.1 = (bf16[8,64,128]{2,1,0:T(8,128)(2,1)S(1)}, bf16[8,64,128]{2,1,0:T(8,128)(2,1)S(1)}, u32[]{:S(2)}, u32[]{:S(2)}) collective-permute-start(bf16[8,64,128]{2,1,0:T(8,128)(2,1)S(1)} %get-tuple-element.19), channel_id=1, source_target_pairs={{0,12},{1,13},{2,14},{3,15},{4,8},{5,9},{6,10},{7,11},{8,4},{9,5},... | collective-permute-start | bytes 393224 | tf_op jit(solution)/shard_map/ppermute | solution.py:317
  17.8 0.0 collective-permute-done.4.refs_1_.two_r
  17.8 0.0 copy-start.2
  17.9 0.0 copy-start.1
  17.9 3.3 %collective-permute-start.5 = (bf16[4,128,128]{2,1,0:T(8,128)(2,1)S(1)}, bf16[4,128,128]{2,1,0:T(8,128)(2,1)S(1)}, u32[]{:S(2)}, u32[]{:S(2)}) collective-permute-start(bf16[4,128,128]{2,1,0:T(8,128)(2,1)S(1)} %get-tuple-element.23), channel_id=1, source_target_pairs={{0,16},{16,0},{32,48},{48,32},{64,80},{80,64},{96,112},{112,96},{1... | collective-permute-start | bytes 393224 | tf_op jit(solution)/shard_map/ppermute | solution.py:320
  21.2 3.8 %collective-permute-start.6 = (bf16[4,128,128]{2,1,0:T(8,128)(2,1)S(1)}, bf16[4,128,128]{2,1,0:T(8,128)(2,1)S(1)}, u32[]{:S(2)}, u32[]{:S(2)}) collective-permute-start(bf16[4,128,128]{2,1,0:T(8,128)(2,1)S(1)} %get-tuple-element.24), channel_id=1, source_target_pairs={{16,32},{32,16},{48,64},{64,48},{80,96},{96,80},{112,128},{128,112... | collective-permute-start | bytes 393224 | tf_op jit(solution)/shard_map/ppermute | solution.py:323
  24.9 0.3 collective-permute-done.refs_0_.refs_1_.one_r
  25.2 1.2 %collective-permute-done.1.refs_1_.refs_2_.three_r = bf16[8,64,128]{2,1,0:T(8,128)(2,1)S(1)} collective-permute-done((bf16[8,64,128]{2,1,0:T(8,128)(2,1)S(1)}, bf16[8,64,128]{2,1,0:T(8,128)(2,1)S(1)}, u32[]{:S(2)}, u32[]{:S(2)}) %collective-permute-start.1) | collective-permute-done | bytes 131104 | tf_op jit(solution)/shard_map/ppermute | solution.py:317
  26.5 3.4 %collective-permute-start.2 = (bf16[4,128,128]{2,1,0:T(8,128)(2,1)S(1)}, bf16[4,128,128]{2,1,0:T(8,128)(2,1)S(1)}, u32[]{:S(2)}, u32[]{:S(2)}) collective-permute-start(bf16[4,128,128]{2,1,0:T(8,128)(2,1)S(1)} %get-tuple-element.20), channel_id=1, source_target_pairs={{0,16},{16,0},{32,48},{48,32},{64,80},{80,64},{96,112},{112,96},{1... | collective-permute-start | bytes 393224 | tf_op jit(solution)/shard_map/ppermute | solution.py:320
  29.9 3.8 %collective-permute-start.3 = (bf16[4,128,128]{2,1,0:T(8,128)(2,1)S(1)}, bf16[4,128,128]{2,1,0:T(8,128)(2,1)S(1)}, u32[]{:S(2)}, u32[]{:S(2)}) collective-permute-start(bf16[4,128,128]{2,1,0:T(8,128)(2,1)S(1)} %get-tuple-element.21), channel_id=1, source_target_pairs={{16,32},{32,16},{48,64},{64,48},{80,96},{96,80},{112,128},{128,112... | collective-permute-start | bytes 393224 | tf_op jit(solution)/shard_map/ppermute | solution.py:323
  33.6 0.0 copy-done.2
  33.6 0.0 copy-done.1
  33.6 0.1 weights.1
  33.8 0.0 collective-permute-done.5.near_r
  33.8 0.0 collective-permute-done.6.far_r
  33.8 0.0 copy-start.3
  33.8 0.0 copy-start.4
  33.8 0.6 %copy-done.3 = f32[64]{0:T(128)S(1)} copy-done((f32[64]{0:T(128)S(1)}, f32[64]{0:T(128)}, u32[]{:S(2)}) %copy-start.3) | copy-done | bytes 280
  34.5 0.0 copy-done.4
  34.5 1.0 %merge_own.1.refs_3_.mine_r = bf16[12,64,128]{2,1,0:T(8,128)(2,1)S(1)} custom-call(bf16[4,128,128]{2,1,0:T(8,128)(2,1)S(1)} %collective-permute-done.5.near_r, bf16[4,128,128]{2,1,0:T(8,128)(2,1)S(1)} %collective-permute-done.6.far_r, bf16[8,64,128]{2,1,0:T(8,128)(2,1)S(1)} %get-tuple-element.22.refs_0_.own_r, ...), custom_call_target="tpu_custom_call" | custom-call | tf_op jit(solution)/shard_map/merge_own/pallas_call | solution.py:208
  35.5 0.0 collective-permute-done.2.refs_0_.near_r
  35.5 1.5 %merge_inner.1 = (bf16[2,64,128]{2,1,0:T(8,128)(2,1)S(1)}, bf16[2,128,128]{2,1,0:T(8,128)(2,1)S(1)}, bf16[2,64,128]{2,1,0:T(8,128)(2,1)S(1)}, f32[4,64,128]{2,1,0:T(8,128)S(1)}) custom-call(bf16[4,128,128]{2,1,0:T(8,128)(2,1)S(1)} %collective-permute-done.2.refs_0_.near_r, bf16[8,64,128]{2,1,0:T(8,128)(2,1)S(1)} %collective-permute-done.refs_0_.refs_1_.one_r, ...), custom_call_target="tpu_custom_call" | custom-call | tf_op jit(solution)/shard_map/merge_inner/pallas_call | solution.py:240
  37.0 2.8 %collective-permute-done.3.far_r = bf16[4,128,128]{2,1,0:T(8,128)(2,1)S(1)} collective-permute-done((bf16[4,128,128]{2,1,0:T(8,128)(2,1)S(1)}, bf16[4,128,128]{2,1,0:T(8,128)(2,1)S(1)}, u32[]{:S(2)}, u32[]{:S(2)}) %collective-permute-start.3) | collective-permute-done | bytes 131104 | tf_op jit(solution)/shard_map/ppermute | solution.py:323
  39.8 2.0 %merge_outer.1 = bf16[64,8,128]{2,1,0:T(8,128)(2,1)} custom-call(bf16[4,128,128]{2,1,0:T(8,128)(2,1)S(1)} %collective-permute-done.2.refs_0_.near_r, bf16[4,128,128]{2,1,0:T(8,128)(2,1)S(1)} %collective-permute-done.3.far_r, bf16[8,64,128]{2,1,0:T(8,128)(2,1)S(1)} %collective-permute-done.refs_0_.refs_1_.one_r, ...), custom_call_target="tpu_custom_call" | custom-call | tf_op jit(solution)/shard_map/merge_outer/pallas_call | solution.py:294
  (2 shorter events, 0.0 us)
Async XLA Ops:
  0.0 11.7 %copy-start = (bf16[4,64,8,128]{3,2,1,0:T(8,128)(2,1)S(1)}, bf16[4,64,8,128]{3,2,1,0:T(8,128)(2,1)}, u32[]{:S(2)}) copy-start(bf16[4,64,8,128]{3,2,1,0:T(8,128)(2,1)} %src.3) | copy-start | bytes 1572868
  1.0 16.8 %collective-permute-start.4 = (bf16[8,64,128]{2,1,0:T(8,128)(2,1)S(1)}, bf16[8,64,128]{2,1,0:T(8,128)(2,1)S(1)}, u32[]{:S(2)}, u32[]{:S(2)}) collective-permute-start(bf16[8,64,128]{2,1,0:T(8,128)(2,1)S(1)} %lead.1), channel_id=1, source_target_pairs={{0,8},{1,9},{2,10},{3,11},{4,12},{5,13},{6,14},{7,15},{8,0},{9,1},... | collective-permute-start | bytes 393224 | tf_op jit(solution)/shard_map/ppermute | solution.py:317
  11.9 13.3 %collective-permute-start = (bf16[8,64,128]{2,1,0:T(8,128)(2,1)S(1)}, bf16[8,64,128]{2,1,0:T(8,128)(2,1)S(1)}, u32[]{:S(2)}, u32[]{:S(2)}) collective-permute-start(bf16[8,64,128]{2,1,0:T(8,128)(2,1)S(1)} %get-tuple-element.18), channel_id=1, source_target_pairs={{0,4},{1,5},{2,6},{3,7},{4,0},{5,1},{6,2},{7,3},{8,12},{9,13},{10,... | collective-permute-start | bytes 393224 | tf_op jit(solution)/shard_map/ppermute | solution.py:317
  15.9 10.5 %collective-permute-start.1 = (bf16[8,64,128]{2,1,0:T(8,128)(2,1)S(1)}, bf16[8,64,128]{2,1,0:T(8,128)(2,1)S(1)}, u32[]{:S(2)}, u32[]{:S(2)}) collective-permute-start(bf16[8,64,128]{2,1,0:T(8,128)(2,1)S(1)} %get-tuple-element.19), channel_id=1, source_target_pairs={{0,12},{1,13},{2,14},{3,15},{4,8},{5,9},{6,10},{7,11},{8,4},{9,5},... | collective-permute-start | bytes 393224 | tf_op jit(solution)/shard_map/ppermute | solution.py:317
  17.8 15.8 %copy-start.2 = (bf16[3,3,64,64]{3,2,1,0:T(8,128)(2,1)S(1)}, bf16[3,3,64,64]{3,2,1,0:T(8,128)(2,1)}, u32[]{:S(2)}) copy-start(bf16[3,3,64,64]{3,2,1,0:T(8,128)(2,1)} %param.7) | copy-start | bytes 221188
  17.9 15.7 %copy-start.1 = (bf16[3,3,64,128]{3,2,1,0:T(8,128)(2,1)S(1)}, bf16[3,3,64,128]{3,2,1,0:T(8,128)(2,1)}, u32[]{:S(2)}) copy-start(bf16[3,3,64,128]{3,2,1,0:T(8,128)(2,1)} %param.6) | copy-start | bytes 442372
  17.9 15.9 %collective-permute-start.5 = (bf16[4,128,128]{2,1,0:T(8,128)(2,1)S(1)}, bf16[4,128,128]{2,1,0:T(8,128)(2,1)S(1)}, u32[]{:S(2)}, u32[]{:S(2)}) collective-permute-start(bf16[4,128,128]{2,1,0:T(8,128)(2,1)S(1)} %get-tuple-element.23), channel_id=1, source_target_pairs={{0,16},{16,0},{32,48},{48,32},{64,80},{80,64},{96,112},{112,96},{1... | collective-permute-start | bytes 393224 | tf_op jit(solution)/shard_map/ppermute | solution.py:320
  21.2 12.6 %collective-permute-start.6 = (bf16[4,128,128]{2,1,0:T(8,128)(2,1)S(1)}, bf16[4,128,128]{2,1,0:T(8,128)(2,1)S(1)}, u32[]{:S(2)}, u32[]{:S(2)}) collective-permute-start(bf16[4,128,128]{2,1,0:T(8,128)(2,1)S(1)} %get-tuple-element.24), channel_id=1, source_target_pairs={{16,32},{32,16},{48,64},{64,48},{80,96},{96,80},{112,128},{128,112... | collective-permute-start | bytes 393224 | tf_op jit(solution)/shard_map/ppermute | solution.py:323
  26.5 9.0 %collective-permute-start.2 = (bf16[4,128,128]{2,1,0:T(8,128)(2,1)S(1)}, bf16[4,128,128]{2,1,0:T(8,128)(2,1)S(1)}, u32[]{:S(2)}, u32[]{:S(2)}) collective-permute-start(bf16[4,128,128]{2,1,0:T(8,128)(2,1)S(1)} %get-tuple-element.20), channel_id=1, source_target_pairs={{0,16},{16,0},{32,48},{48,32},{64,80},{80,64},{96,112},{112,96},{1... | collective-permute-start | bytes 393224 | tf_op jit(solution)/shard_map/ppermute | solution.py:320
  29.9 9.9 %collective-permute-start.3 = (bf16[4,128,128]{2,1,0:T(8,128)(2,1)S(1)}, bf16[4,128,128]{2,1,0:T(8,128)(2,1)S(1)}, u32[]{:S(2)}, u32[]{:S(2)}) collective-permute-start(bf16[4,128,128]{2,1,0:T(8,128)(2,1)S(1)} %get-tuple-element.21), channel_id=1, source_target_pairs={{16,32},{32,16},{48,64},{64,48},{80,96},{96,80},{112,128},{128,112... | collective-permute-start | bytes 393224 | tf_op jit(solution)/shard_map/ppermute | solution.py:323
  33.8 0.7 %copy-start.3 = (f32[64]{0:T(128)S(1)}, f32[64]{0:T(128)}, u32[]{:S(2)}) copy-start(f32[64]{0:T(128)} %param.8) | copy-start | bytes 772
  33.8 0.7 %copy-start.4 = (f32[64]{0:T(128)S(1)}, f32[64]{0:T(128)}, u32[]{:S(2)}) copy-start(f32[64]{0:T(128)} %param.9) | copy-start | bytes 772
